TPU v7x, 32 devices: a whole 2x2x4 slice. The times are simulated.
32 devices in a mesh: depth: 8 (over z, x), imgy: 2 (over y), imgx: 2 (over core).
Axes of the slice: x: 2, y: 2, z: 4, core: 2. Of those that a mesh axis runs over, the one named last changes fastest.
Arguments:
- volume: bfloat16 [128, 512, 1024], P('depth', 'imgy', 'imgx'), may hold values from -6 to 6
- tf_centers: float32 [4], replicated, may hold values from -2 to 2
- tf_widths: float32 [4], replicated, may hold values from 0.4 to 1.5
- tf_colors: float32 [3, 4], replicated, may hold values from 0.2 to 3
- tf_opacity: float32 [4], replicated, may hold values from 0.3 to 3
Outputs:
- frame: float32 [4, 2, 256, 1024], P(None, 'imgy', 'depth', 'imgx')
All inputs are finite; a program needn't handle non-finite values.
Results may differ from a plain program's by a relative error of at most 0.0003.
Values may be sent and summed in bfloat16 or wider, within the bound.
A program may use at most 64 MiB of HBM per device.

v0:
```python
import jax
import jax.numpy as jnp
from jax import lax
from jax.sharding import PartitionSpec as P


def extended(block, sides, width):
    for axis, dim in sides:
        count = lax.axis_size(axis)
        forward = [(i, i + 1) for i in range(count - 1)]
        backward = [(target, source) for source, target in forward]
        low = lax.ppermute(
            lax.slice_in_dim(block, block.shape[dim] - width, None, axis=dim), axis, forward
        )
        high = lax.ppermute(lax.slice_in_dim(block, 0, width, axis=dim), axis, backward)
        block = jnp.concatenate([low, block, high], axis=dim)
    return block


def partner(array, axis, distance):
    return lax.ppermute(array, axis, [(i, i ^ 1 << distance) for i in range(lax.axis_size(axis))])


def shading(
    middle, grad_depth, grad_rows, grad_cols, tf_centers, tf_widths, tf_colors, tf_opacity, ray_step
):
    extinction = jnp.zeros_like(middle)
    emission = [jnp.zeros_like(middle), jnp.zeros_like(middle), jnp.zeros_like(middle)]
    for bump_index in range(tf_centers.shape[0]):
        offset = (middle - tf_centers[bump_index]) / tf_widths[bump_index]
        profile = jnp.exp(-offset * offset)
        extinction = extinction + tf_opacity[bump_index] * profile
        for channel in range(3):
            emission[channel] = emission[channel] + tf_colors[channel, bump_index] * profile
    gradient_norm = jnp.sqrt(
        grad_depth * grad_depth + grad_rows * grad_rows + grad_cols * grad_cols + 0.25
    )
    lighting = 0.3 + 0.7 * jnp.abs(grad_depth) / gradient_norm
    passing = jnp.exp(-ray_step * extinction)
    weight = (1.0 - passing) * lighting
    glowing = jnp.stack([emitted * weight for emitted in emission])
    return (glowing, passing)


def over_merge(nearer, farther, channel_axis):
    near_color = lax.slice_in_dim(nearer, 0, 3, axis=channel_axis)
    near_passed = lax.slice_in_dim(nearer, 3, 4, axis=channel_axis)
    far_color = lax.slice_in_dim(farther, 0, 3, axis=channel_axis)
    far_passed = lax.slice_in_dim(farther, 3, 4, axis=channel_axis)
    color_part = near_color + near_passed * far_color
    passed_part = near_passed * far_passed
    return jnp.concatenate([color_part, passed_part], axis=channel_axis)


def local(volume, tf_centers, tf_widths, tf_colors, tf_opacity):
    slabs = lax.axis_size("depth")
    depth_index = lax.axis_index("depth")
    layers, rows, cols = volume.shape
    ray_step = 1.5 / (layers * slabs)
    piece_rows = rows // slabs
    depth_padded = extended(volume, (("depth", 0),), 1)
    side_padded = extended(volume, (("imgy", 1), ("imgx", 2)), 1)

    def march_layer(carried, inputs):
        color_sum, passed = carried
        before, after, side = inputs
        side = side.astype(jnp.float32)
        middle = side[1:-1, 1:-1]
        grad_depth = 0.5 * (after.astype(jnp.float32) - before.astype(jnp.float32))
        grad_rows = 0.5 * (side[2:, 1:-1] - side[:-2, 1:-1])
        grad_cols = 0.5 * (side[1:-1, 2:] - side[1:-1, :-2])
        glowing, passing = shading(
            middle,
            grad_depth,
            grad_rows,
            grad_cols,
            tf_centers,
            tf_widths,
            tf_colors,
            tf_opacity,
            ray_step,
        )
        return ((color_sum + passed[None] * glowing, passed * passing), None)

    start = (jnp.zeros((3, rows, cols), jnp.float32), jnp.ones((rows, cols), jnp.float32))
    final, unused = lax.scan(march_layer, start, (depth_padded[:-2], depth_padded[2:], side_padded))
    color_sum, passed = final
    partial_value = jnp.concatenate([color_sum, passed[None]], axis=0)
    rounds = slabs.bit_length() - 1
    for bit_number in range(rounds):
        pieces_left = partial_value.shape[1] // piece_rows
        grouped = partial_value.reshape(4, pieces_left // 2, 2, piece_rows, cols)
        own_bit = depth_index // 2**bit_number % 2
        kept_half = lax.dynamic_index_in_dim(grouped, own_bit, 2, keepdims=False)
        sent_half = lax.dynamic_index_in_dim(grouped, 1 - own_bit, 2, keepdims=False)
        received = partner(sent_half, "depth", bit_number)
        nearer = jnp.where(own_bit == 0, kept_half, received)
        farther = jnp.where(own_bit == 0, received, kept_half)
        merged = over_merge(nearer, farther, 0)
        partial_value = merged.reshape(4, pieces_left // 2 * piece_rows, cols)
    frame = jnp.concatenate([partial_value[:3], 1.0 - partial_value[3:4]], axis=0)
    return frame[:, None]


def solution(mesh):
    in_specs = (P("depth", "imgy", "imgx"), P(), P(), P(), P())
    out_specs = P(None, "imgy", "depth", "imgx")
    return jax.shard_map(local, mesh=mesh, in_specs=in_specs, out_specs=out_specs, check_vma=False)
```

profile of v0, /device:TPU:0, one launch (start us, length us, event | category | flops | bytes accessed | tf_op | source)
XLA Modules:
  0.0 731.2 jit_solution(8036977006316562687)
XLA Ops:
  1.0 4.9 collective-permute-start
  7.2 7.9 %copy.17 = bf16[16,256,512]{1,0,2:T(8,128)(2,1)} copy(bf16[16,256,512]{2,1,0:T(8,128)(2,1)} %param.7) | data formatting | bytes 8388608 | tf_op args[0]
  15.2 2.1 copy.16
  17.2 2.9 copy.18
  26.1 4.6 collective-permute-start.5
  30.8 9.7 %pad_maximum_fusion = bf16[16,258,514]{1,0,2:T(8,128)(2,1)} fusion(bf16[16,258,1]{1,0,2:T(8,128)(2,1)S(1)} %collective-permute-done.3, bf16[16,1,512]{1,0,2:T(8,128)(2,1)} %copy.18, bf16[16,256,512]{1,0,2:T(8,128)(2,1)} %copy.17, bf16[16,1,512]{1,0,2:T(8,128)(2,1)} %copy-done, bf16[16,258,1]{1,0,2:T(8,128)(2,1)S(1)} %collective-permute-done.2), kind=kLoop, calls=%fused_computation.30 | loop fusion | flops 21217920 | bytes 8487168 | tf_op jit(solution)/shard_map/concatenate | solution.py:16
  40.5 9.6 %copy.19 = bf16[16,258,514]{2,1,0:T(8,128)(2,1)} copy(bf16[16,258,514]{1,0,2:T(8,128)(2,1)} %pad_maximum_fusion) | data formatting | bytes 8487168
  50.1 5.9 pad_maximum_fusion.1
  56.0 616.7 %while.13 = (s32[]{:T(128)}, f32[3,256,512]{2,1,0:T(8,128)S(1)}, f32[256,512]{1,0:T(8,128)}, f32[3,4]{1,0:T(4,128)S(1)}, bf16[16,258,514]{2,1,0:T(8,128)(2,1)}, ...) while((s32[]{:T(128)}, f32[3,256,512]{2,1,0:T(8,128)S(1)}, ...), condition=%wide.region_1.2_spmd.clone, body=%wide.region_0.1_spmd.clone.sunk | while | flops 16516615 | bytes 14427664 | solution.py:86
  59.1 12.2 %multiply_bitcast_fusion.5 = (f32[1,256,512]{2,1,0:T(8,128)S(1)}, f32[256,512]{1,0:T(8,128)S(1)}) fusion(f32[]{:T(128)} %bitcast.101, f32[]{:T(128)} %bitcast.102, f32[]{:T(128)} %bitcast.103, f32[]{:T(128)} %bitcast.104, f32[]{:T(128)} %bitcast.105, f32[]{:T(128)} %bitcast.106, f32[258,514]{1,0:T(8,128)S(1)} %bitcast_convert_fusion.2, f32[]{:T(128)} %bitcast.107, ...), kind=kLoop, calls=%fused_computation.25.clone.1 | loop fusion | flops 6815744 | bytes 4194372 | tf_op jit(solution)/shard_map/while/body/eval_jaxpr/stack | solution.py:41
  71.3 11.8 %multiply_bitcast_fusion.6 = (f32[1,256,512]{2,1,0:T(8,128)S(1)}, f32[1,256,512]{2,1,0:T(8,128)}) fusion(f32[256,512]{1,0:T(8,128)S(1)} %get-tuple-element.294, f32[]{:T(128)} %bitcast.117, f32[]{:T(128)} %bitcast.118, f32[]{:T(128)} %bitcast.119, f32[]{:T(128)} %bitcast.120, f32[]{:T(128)} %bitcast.105, f32[]{:T(128)} %bitcast.106, ...), kind=kLoop, calls=%fused_computation.24.clone.1 | loop fusion | flops 4194304 | bytes 2097216 | tf_op jit(solution)/shard_map/while/body/eval_jaxpr/stack | solution.py:41
  83.0 9.0 %fusion.44 = (f32[256,512]{1,0:T(8,128)}, f32[256,512]{1,0:T(8,128)S(1)}) fusion(f32[]{:T(128)} %bitcast.105, f32[]{:T(128)} %bitcast.106, f32[]{:T(128)} %bitcast.113, f32[]{:T(128)} %bitcast.107, f32[]{:T(128)} %bitcast.108, f32[]{:T(128)} %bitcast.114, f32[]{:T(128)} %bitcast.109, f32[]{:T(128)} %bitcast.110, f32[]{:T(128)} %bitcast.115, ...), kind=kLoop, calls=%fused_computation.29.clone.1 | loop fusion | flops 3407872 | bytes 2097201 | tf_op jit(solution)/shard_map/while/body/eval_jaxpr/mul | solution.py:83
  96.7 12.2 %multiply_bitcast_fusion.5 = (f32[1,256,512]{2,1,0:T(8,128)S(1)}, f32[256,512]{1,0:T(8,128)S(1)}) fusion(f32[]{:T(128)} %bitcast.101, f32[]{:T(128)} %bitcast.102, f32[]{:T(128)} %bitcast.103, f32[]{:T(128)} %bitcast.104, f32[]{:T(128)} %bitcast.105, f32[]{:T(128)} %bitcast.106, f32[258,514]{1,0:T(8,128)S(1)} %bitcast_convert_fusion.2, f32[]{:T(128)} %bitcast.107, ...), kind=kLoop, calls=%fused_computation.25.clone.1 | loop fusion | flops 6815744 | bytes 4194372 | tf_op jit(solution)/shard_map/while/body/eval_jaxpr/stack | solution.py:41
  108.9 11.8 %multiply_bitcast_fusion.6 = (f32[1,256,512]{2,1,0:T(8,128)S(1)}, f32[1,256,512]{2,1,0:T(8,128)}) fusion(f32[256,512]{1,0:T(8,128)S(1)} %get-tuple-element.294, f32[]{:T(128)} %bitcast.117, f32[]{:T(128)} %bitcast.118, f32[]{:T(128)} %bitcast.119, f32[]{:T(128)} %bitcast.120, f32[]{:T(128)} %bitcast.105, f32[]{:T(128)} %bitcast.106, ...), kind=kLoop, calls=%fused_computation.24.clone.1 | loop fusion | flops 4194304 | bytes 2097216 | tf_op jit(solution)/shard_map/while/body/eval_jaxpr/stack | solution.py:41
  120.6 10.0 %fusion.44 = (f32[256,512]{1,0:T(8,128)}, f32[256,512]{1,0:T(8,128)S(1)}) fusion(f32[]{:T(128)} %bitcast.105, f32[]{:T(128)} %bitcast.106, f32[]{:T(128)} %bitcast.113, f32[]{:T(128)} %bitcast.107, f32[]{:T(128)} %bitcast.108, f32[]{:T(128)} %bitcast.114, f32[]{:T(128)} %bitcast.109, f32[]{:T(128)} %bitcast.110, f32[]{:T(128)} %bitcast.115, ...), kind=kLoop, calls=%fused_computation.29.clone.1 | loop fusion | flops 3407872 | bytes 2097201 | tf_op jit(solution)/shard_map/while/body/eval_jaxpr/mul | solution.py:83
  135.3 12.2 %multiply_bitcast_fusion.5 = (f32[1,256,512]{2,1,0:T(8,128)S(1)}, f32[256,512]{1,0:T(8,128)S(1)}) fusion(f32[]{:T(128)} %bitcast.101, f32[]{:T(128)} %bitcast.102, f32[]{:T(128)} %bitcast.103, f32[]{:T(128)} %bitcast.104, f32[]{:T(128)} %bitcast.105, f32[]{:T(128)} %bitcast.106, f32[258,514]{1,0:T(8,128)S(1)} %bitcast_convert_fusion.2, f32[]{:T(128)} %bitcast.107, ...), kind=kLoop, calls=%fused_computation.25.clone.1 | loop fusion | flops 6815744 | bytes 4194372 | tf_op jit(solution)/shard_map/while/body/eval_jaxpr/stack | solution.py:41
  147.5 11.8 %multiply_bitcast_fusion.6 = (f32[1,256,512]{2,1,0:T(8,128)S(1)}, f32[1,256,512]{2,1,0:T(8,128)}) fusion(f32[256,512]{1,0:T(8,128)S(1)} %get-tuple-element.294, f32[]{:T(128)} %bitcast.117, f32[]{:T(128)} %bitcast.118, f32[]{:T(128)} %bitcast.119, f32[]{:T(128)} %bitcast.120, f32[]{:T(128)} %bitcast.105, f32[]{:T(128)} %bitcast.106, ...), kind=kLoop, calls=%fused_computation.24.clone.1 | loop fusion | flops 4194304 | bytes 2097216 | tf_op jit(solution)/shard_map/while/body/eval_jaxpr/stack | solution.py:41
  159.2 10.0 %fusion.44 = (f32[256,512]{1,0:T(8,128)}, f32[256,512]{1,0:T(8,128)S(1)}) fusion(f32[]{:T(128)} %bitcast.105, f32[]{:T(128)} %bitcast.106, f32[]{:T(128)} %bitcast.113, f32[]{:T(128)} %bitcast.107, f32[]{:T(128)} %bitcast.108, f32[]{:T(128)} %bitcast.114, f32[]{:T(128)} %bitcast.109, f32[]{:T(128)} %bitcast.110, f32[]{:T(128)} %bitcast.115, ...), kind=kLoop, calls=%fused_computation.29.clone.1 | loop fusion | flops 3407872 | bytes 2097201 | tf_op jit(solution)/shard_map/while/body/eval_jaxpr/mul | solution.py:83
  173.9 12.2 %multiply_bitcast_fusion.5 = (f32[1,256,512]{2,1,0:T(8,128)S(1)}, f32[256,512]{1,0:T(8,128)S(1)}) fusion(f32[]{:T(128)} %bitcast.101, f32[]{:T(128)} %bitcast.102, f32[]{:T(128)} %bitcast.103, f32[]{:T(128)} %bitcast.104, f32[]{:T(128)} %bitcast.105, f32[]{:T(128)} %bitcast.106, f32[258,514]{1,0:T(8,128)S(1)} %bitcast_convert_fusion.2, f32[]{:T(128)} %bitcast.107, ...), kind=kLoop, calls=%fused_computation.25.clone.1 | loop fusion | flops 6815744 | bytes 4194372 | tf_op jit(solution)/shard_map/while/body/eval_jaxpr/stack | solution.py:41
  186.1 11.8 %multiply_bitcast_fusion.6 = (f32[1,256,512]{2,1,0:T(8,128)S(1)}, f32[1,256,512]{2,1,0:T(8,128)}) fusion(f32[256,512]{1,0:T(8,128)S(1)} %get-tuple-element.294, f32[]{:T(128)} %bitcast.117, f32[]{:T(128)} %bitcast.118, f32[]{:T(128)} %bitcast.119, f32[]{:T(128)} %bitcast.120, f32[]{:T(128)} %bitcast.105, f32[]{:T(128)} %bitcast.106, ...), kind=kLoop, calls=%fused_computation.24.clone.1 | loop fusion | flops 4194304 | bytes 2097216 | tf_op jit(solution)/shard_map/while/body/eval_jaxpr/stack | solution.py:41
  197.8 10.0 %fusion.44 = (f32[256,512]{1,0:T(8,128)}, f32[256,512]{1,0:T(8,128)S(1)}) fusion(f32[]{:T(128)} %bitcast.105, f32[]{:T(128)} %bitcast.106, f32[]{:T(128)} %bitcast.113, f32[]{:T(128)} %bitcast.107, f32[]{:T(128)} %bitcast.108, f32[]{:T(128)} %bitcast.114, f32[]{:T(128)} %bitcast.109, f32[]{:T(128)} %bitcast.110, f32[]{:T(128)} %bitcast.115, ...), kind=kLoop, calls=%fused_computation.29.clone.1 | loop fusion | flops 3407872 | bytes 2097201 | tf_op jit(solution)/shard_map/while/body/eval_jaxpr/mul | solution.py:83
  212.5 12.2 %multiply_bitcast_fusion.5 = (f32[1,256,512]{2,1,0:T(8,128)S(1)}, f32[256,512]{1,0:T(8,128)S(1)}) fusion(f32[]{:T(128)} %bitcast.101, f32[]{:T(128)} %bitcast.102, f32[]{:T(128)} %bitcast.103, f32[]{:T(128)} %bitcast.104, f32[]{:T(128)} %bitcast.105, f32[]{:T(128)} %bitcast.106, f32[258,514]{1,0:T(8,128)S(1)} %bitcast_convert_fusion.2, f32[]{:T(128)} %bitcast.107, ...), kind=kLoop, calls=%fused_computation.25.clone.1 | loop fusion | flops 6815744 | bytes 4194372 | tf_op jit(solution)/shard_map/while/body/eval_jaxpr/stack | solution.py:41
  224.7 11.8 %multiply_bitcast_fusion.6 = (f32[1,256,512]{2,1,0:T(8,128)S(1)}, f32[1,256,512]{2,1,0:T(8,128)}) fusion(f32[256,512]{1,0:T(8,128)S(1)} %get-tuple-element.294, f32[]{:T(128)} %bitcast.117, f32[]{:T(128)} %bitcast.118, f32[]{:T(128)} %bitcast.119, f32[]{:T(128)} %bitcast.120, f32[]{:T(128)} %bitcast.105, f32[]{:T(128)} %bitcast.106, ...), kind=kLoop, calls=%fused_computation.24.clone.1 | loop fusion | flops 4194304 | bytes 2097216 | tf_op jit(solution)/shard_map/while/body/eval_jaxpr/stack | solution.py:41
  236.4 10.0 %fusion.44 = (f32[256,512]{1,0:T(8,128)}, f32[256,512]{1,0:T(8,128)S(1)}) fusion(f32[]{:T(128)} %bitcast.105, f32[]{:T(128)} %bitcast.106, f32[]{:T(128)} %bitcast.113, f32[]{:T(128)} %bitcast.107, f32[]{:T(128)} %bitcast.108, f32[]{:T(128)} %bitcast.114, f32[]{:T(128)} %bitcast.109, f32[]{:T(128)} %bitcast.110, f32[]{:T(128)} %bitcast.115, ...), kind=kLoop, calls=%fused_computation.29.clone.1 | loop fusion | flops 3407872 | bytes 2097201 | tf_op jit(solution)/shard_map/while/body/eval_jaxpr/mul | solution.py:83
  251.1 12.2 %multiply_bitcast_fusion.5 = (f32[1,256,512]{2,1,0:T(8,128)S(1)}, f32[256,512]{1,0:T(8,128)S(1)}) fusion(f32[]{:T(128)} %bitcast.101, f32[]{:T(128)} %bitcast.102, f32[]{:T(128)} %bitcast.103, f32[]{:T(128)} %bitcast.104, f32[]{:T(128)} %bitcast.105, f32[]{:T(128)} %bitcast.106, f32[258,514]{1,0:T(8,128)S(1)} %bitcast_convert_fusion.2, f32[]{:T(128)} %bitcast.107, ...), kind=kLoop, calls=%fused_computation.25.clone.1 | loop fusion | flops 6815744 | bytes 4194372 | tf_op jit(solution)/shard_map/while/body/eval_jaxpr/stack | solution.py:41
  263.3 11.8 %multiply_bitcast_fusion.6 = (f32[1,256,512]{2,1,0:T(8,128)S(1)}, f32[1,256,512]{2,1,0:T(8,128)}) fusion(f32[256,512]{1,0:T(8,128)S(1)} %get-tuple-element.294, f32[]{:T(128)} %bitcast.117, f32[]{:T(128)} %bitcast.118, f32[]{:T(128)} %bitcast.119, f32[]{:T(128)} %bitcast.120, f32[]{:T(128)} %bitcast.105, f32[]{:T(128)} %bitcast.106, ...), kind=kLoop, calls=%fused_computation.24.clone.1 | loop fusion | flops 4194304 | bytes 2097216 | tf_op jit(solution)/shard_map/while/body/eval_jaxpr/stack | solution.py:41
  275.1 10.0 %fusion.44 = (f32[256,512]{1,0:T(8,128)}, f32[256,512]{1,0:T(8,128)S(1)}) fusion(f32[]{:T(128)} %bitcast.105, f32[]{:T(128)} %bitcast.106, f32[]{:T(128)} %bitcast.113, f32[]{:T(128)} %bitcast.107, f32[]{:T(128)} %bitcast.108, f32[]{:T(128)} %bitcast.114, f32[]{:T(128)} %bitcast.109, f32[]{:T(128)} %bitcast.110, f32[]{:T(128)} %bitcast.115, ...), kind=kLoop, calls=%fused_computation.29.clone.1 | loop fusion | flops 3407872 | bytes 2097201 | tf_op jit(solution)/shard_map/while/body/eval_jaxpr/mul | solution.py:83
  289.7 12.2 %multiply_bitcast_fusion.5 = (f32[1,256,512]{2,1,0:T(8,128)S(1)}, f32[256,512]{1,0:T(8,128)S(1)}) fusion(f32[]{:T(128)} %bitcast.101, f32[]{:T(128)} %bitcast.102, f32[]{:T(128)} %bitcast.103, f32[]{:T(128)} %bitcast.104, f32[]{:T(128)} %bitcast.105, f32[]{:T(128)} %bitcast.106, f32[258,514]{1,0:T(8,128)S(1)} %bitcast_convert_fusion.2, f32[]{:T(128)} %bitcast.107, ...), kind=kLoop, calls=%fused_computation.25.clone.1 | loop fusion | flops 6815744 | bytes 4194372 | tf_op jit(solution)/shard_map/while/body/eval_jaxpr/stack | solution.py:41
  301.9 11.8 %multiply_bitcast_fusion.6 = (f32[1,256,512]{2,1,0:T(8,128)S(1)}, f32[1,256,512]{2,1,0:T(8,128)}) fusion(f32[256,512]{1,0:T(8,128)S(1)} %get-tuple-element.294, f32[]{:T(128)} %bitcast.117, f32[]{:T(128)} %bitcast.118, f32[]{:T(128)} %bitcast.119, f32[]{:T(128)} %bitcast.120, f32[]{:T(128)} %bitcast.105, f32[]{:T(128)} %bitcast.106, ...), kind=kLoop, calls=%fused_computation.24.clone.1 | loop fusion | flops 4194304 | bytes 2097216 | tf_op jit(solution)/shard_map/while/body/eval_jaxpr/stack | solution.py:41
  313.7 10.0 %fusion.44 = (f32[256,512]{1,0:T(8,128)}, f32[256,512]{1,0:T(8,128)S(1)}) fusion(f32[]{:T(128)} %bitcast.105, f32[]{:T(128)} %bitcast.106, f32[]{:T(128)} %bitcast.113, f32[]{:T(128)} %bitcast.107, f32[]{:T(128)} %bitcast.108, f32[]{:T(128)} %bitcast.114, f32[]{:T(128)} %bitcast.109, f32[]{:T(128)} %bitcast.110, f32[]{:T(128)} %bitcast.115, ...), kind=kLoop, calls=%fused_computation.29.clone.1 | loop fusion | flops 3407872 | bytes 2097201 | tf_op jit(solution)/shard_map/while/body/eval_jaxpr/mul | solution.py:83
  328.3 12.2 %multiply_bitcast_fusion.5 = (f32[1,256,512]{2,1,0:T(8,128)S(1)}, f32[256,512]{1,0:T(8,128)S(1)}) fusion(f32[]{:T(128)} %bitcast.101, f32[]{:T(128)} %bitcast.102, f32[]{:T(128)} %bitcast.103, f32[]{:T(128)} %bitcast.104, f32[]{:T(128)} %bitcast.105, f32[]{:T(128)} %bitcast.106, f32[258,514]{1,0:T(8,128)S(1)} %bitcast_convert_fusion.2, f32[]{:T(128)} %bitcast.107, ...), kind=kLoop, calls=%fused_computation.25.clone.1 | loop fusion | flops 6815744 | bytes 4194372 | tf_op jit(solution)/shard_map/while/body/eval_jaxpr/stack | solution.py:41
  340.5 11.8 %multiply_bitcast_fusion.6 = (f32[1,256,512]{2,1,0:T(8,128)S(1)}, f32[1,256,512]{2,1,0:T(8,128)}) fusion(f32[256,512]{1,0:T(8,128)S(1)} %get-tuple-element.294, f32[]{:T(128)} %bitcast.117, f32[]{:T(128)} %bitcast.118, f32[]{:T(128)} %bitcast.119, f32[]{:T(128)} %bitcast.120, f32[]{:T(128)} %bitcast.105, f32[]{:T(128)} %bitcast.106, ...), kind=kLoop, calls=%fused_computation.24.clone.1 | loop fusion | flops 4194304 | bytes 2097216 | tf_op jit(solution)/shard_map/while/body/eval_jaxpr/stack | solution.py:41
  352.3 10.0 %fusion.44 = (f32[256,512]{1,0:T(8,128)}, f32[256,512]{1,0:T(8,128)S(1)}) fusion(f32[]{:T(128)} %bitcast.105, f32[]{:T(128)} %bitcast.106, f32[]{:T(128)} %bitcast.113, f32[]{:T(128)} %bitcast.107, f32[]{:T(128)} %bitcast.108, f32[]{:T(128)} %bitcast.114, f32[]{:T(128)} %bitcast.109, f32[]{:T(128)} %bitcast.110, f32[]{:T(128)} %bitcast.115, ...), kind=kLoop, calls=%fused_computation.29.clone.1 | loop fusion | flops 3407872 | bytes 2097201 | tf_op jit(solution)/shard_map/while/body/eval_jaxpr/mul | solution.py:83
  366.9 12.2 %multiply_bitcast_fusion.5 = (f32[1,256,512]{2,1,0:T(8,128)S(1)}, f32[256,512]{1,0:T(8,128)S(1)}) fusion(f32[]{:T(128)} %bitcast.101, f32[]{:T(128)} %bitcast.102, f32[]{:T(128)} %bitcast.103, f32[]{:T(128)} %bitcast.104, f32[]{:T(128)} %bitcast.105, f32[]{:T(128)} %bitcast.106, f32[258,514]{1,0:T(8,128)S(1)} %bitcast_convert_fusion.2, f32[]{:T(128)} %bitcast.107, ...), kind=kLoop, calls=%fused_computation.25.clone.1 | loop fusion | flops 6815744 | bytes 4194372 | tf_op jit(solution)/shard_map/while/body/eval_jaxpr/stack | solution.py:41
  379.1 11.8 %multiply_bitcast_fusion.6 = (f32[1,256,512]{2,1,0:T(8,128)S(1)}, f32[1,256,512]{2,1,0:T(8,128)}) fusion(f32[256,512]{1,0:T(8,128)S(1)} %get-tuple-element.294, f32[]{:T(128)} %bitcast.117, f32[]{:T(128)} %bitcast.118, f32[]{:T(128)} %bitcast.119, f32[]{:T(128)} %bitcast.120, f32[]{:T(128)} %bitcast.105, f32[]{:T(128)} %bitcast.106, ...), kind=kLoop, calls=%fused_computation.24.clone.1 | loop fusion | flops 4194304 | bytes 2097216 | tf_op jit(solution)/shard_map/while/body/eval_jaxpr/stack | solution.py:41
  390.9 10.0 %fusion.44 = (f32[256,512]{1,0:T(8,128)}, f32[256,512]{1,0:T(8,128)S(1)}) fusion(f32[]{:T(128)} %bitcast.105, f32[]{:T(128)} %bitcast.106, f32[]{:T(128)} %bitcast.113, f32[]{:T(128)} %bitcast.107, f32[]{:T(128)} %bitcast.108, f32[]{:T(128)} %bitcast.114, f32[]{:T(128)} %bitcast.109, f32[]{:T(128)} %bitcast.110, f32[]{:T(128)} %bitcast.115, ...), kind=kLoop, calls=%fused_computation.29.clone.1 | loop fusion | flops 3407872 | bytes 2097201 | tf_op jit(solution)/shard_map/while/body/eval_jaxpr/mul | solution.py:83
  405.5 12.2 %multiply_bitcast_fusion.5 = (f32[1,256,512]{2,1,0:T(8,128)S(1)}, f32[256,512]{1,0:T(8,128)S(1)}) fusion(f32[]{:T(128)} %bitcast.101, f32[]{:T(128)} %bitcast.102, f32[]{:T(128)} %bitcast.103, f32[]{:T(128)} %bitcast.104, f32[]{:T(128)} %bitcast.105, f32[]{:T(128)} %bitcast.106, f32[258,514]{1,0:T(8,128)S(1)} %bitcast_convert_fusion.2, f32[]{:T(128)} %bitcast.107, ...), kind=kLoop, calls=%fused_computation.25.clone.1 | loop fusion | flops 6815744 | bytes 4194372 | tf_op jit(solution)/shard_map/while/body/eval_jaxpr/stack | solution.py:41
  417.7 11.8 %multiply_bitcast_fusion.6 = (f32[1,256,512]{2,1,0:T(8,128)S(1)}, f32[1,256,512]{2,1,0:T(8,128)}) fusion(f32[256,512]{1,0:T(8,128)S(1)} %get-tuple-element.294, f32[]{:T(128)} %bitcast.117, f32[]{:T(128)} %bitcast.118, f32[]{:T(128)} %bitcast.119, f32[]{:T(128)} %bitcast.120, f32[]{:T(128)} %bitcast.105, f32[]{:T(128)} %bitcast.106, ...), kind=kLoop, calls=%fused_computation.24.clone.1 | loop fusion | flops 4194304 | bytes 2097216 | tf_op jit(solution)/shard_map/while/body/eval_jaxpr/stack | solution.py:41
  429.5 10.0 %fusion.44 = (f32[256,512]{1,0:T(8,128)}, f32[256,512]{1,0:T(8,128)S(1)}) fusion(f32[]{:T(128)} %bitcast.105, f32[]{:T(128)} %bitcast.106, f32[]{:T(128)} %bitcast.113, f32[]{:T(128)} %bitcast.107, f32[]{:T(128)} %bitcast.108, f32[]{:T(128)} %bitcast.114, f32[]{:T(128)} %bitcast.109, f32[]{:T(128)} %bitcast.110, f32[]{:T(128)} %bitcast.115, ...), kind=kLoop, calls=%fused_computation.29.clone.1 | loop fusion | flops 3407872 | bytes 2097201 | tf_op jit(solution)/shard_map/while/body/eval_jaxpr/mul | solution.py:83
  444.1 12.2 %multiply_bitcast_fusion.5 = (f32[1,256,512]{2,1,0:T(8,128)S(1)}, f32[256,512]{1,0:T(8,128)S(1)}) fusion(f32[]{:T(128)} %bitcast.101, f32[]{:T(128)} %bitcast.102, f32[]{:T(128)} %bitcast.103, f32[]{:T(128)} %bitcast.104, f32[]{:T(128)} %bitcast.105, f32[]{:T(128)} %bitcast.106, f32[258,514]{1,0:T(8,128)S(1)} %bitcast_convert_fusion.2, f32[]{:T(128)} %bitcast.107, ...), kind=kLoop, calls=%fused_computation.25.clone.1 | loop fusion | flops 6815744 | bytes 4194372 | tf_op jit(solution)/shard_map/while/body/eval_jaxpr/stack | solution.py:41
  456.3 11.8 %multiply_bitcast_fusion.6 = (f32[1,256,512]{2,1,0:T(8,128)S(1)}, f32[1,256,512]{2,1,0:T(8,128)}) fusion(f32[256,512]{1,0:T(8,128)S(1)} %get-tuple-element.294, f32[]{:T(128)} %bitcast.117, f32[]{:T(128)} %bitcast.118, f32[]{:T(128)} %bitcast.119, f32[]{:T(128)} %bitcast.120, f32[]{:T(128)} %bitcast.105, f32[]{:T(128)} %bitcast.106, ...), kind=kLoop, calls=%fused_computation.24.clone.1 | loop fusion | flops 4194304 | bytes 2097216 | tf_op jit(solution)/shard_map/while/body/eval_jaxpr/stack | solution.py:41
  468.1 10.0 %fusion.44 = (f32[256,512]{1,0:T(8,128)}, f32[256,512]{1,0:T(8,128)S(1)}) fusion(f32[]{:T(128)} %bitcast.105, f32[]{:T(128)} %bitcast.106, f32[]{:T(128)} %bitcast.113, f32[]{:T(128)} %bitcast.107, f32[]{:T(128)} %bitcast.108, f32[]{:T(128)} %bitcast.114, f32[]{:T(128)} %bitcast.109, f32[]{:T(128)} %bitcast.110, f32[]{:T(128)} %bitcast.115, ...), kind=kLoop, calls=%fused_computation.29.clone.1 | loop fusion | flops 3407872 | bytes 2097201 | tf_op jit(solution)/shard_map/while/body/eval_jaxpr/mul | solution.py:83
  482.7 12.2 %multiply_bitcast_fusion.5 = (f32[1,256,512]{2,1,0:T(8,128)S(1)}, f32[256,512]{1,0:T(8,128)S(1)}) fusion(f32[]{:T(128)} %bitcast.101, f32[]{:T(128)} %bitcast.102, f32[]{:T(128)} %bitcast.103, f32[]{:T(128)} %bitcast.104, f32[]{:T(128)} %bitcast.105, f32[]{:T(128)} %bitcast.106, f32[258,514]{1,0:T(8,128)S(1)} %bitcast_convert_fusion.2, f32[]{:T(128)} %bitcast.107, ...), kind=kLoop, calls=%fused_computation.25.clone.1 | loop fusion | flops 6815744 | bytes 4194372 | tf_op jit(solution)/shard_map/while/body/eval_jaxpr/stack | solution.py:41
  494.9 11.8 %multiply_bitcast_fusion.6 = (f32[1,256,512]{2,1,0:T(8,128)S(1)}, f32[1,256,512]{2,1,0:T(8,128)}) fusion(f32[256,512]{1,0:T(8,128)S(1)} %get-tuple-element.294, f32[]{:T(128)} %bitcast.117, f32[]{:T(128)} %bitcast.118, f32[]{:T(128)} %bitcast.119, f32[]{:T(128)} %bitcast.120, f32[]{:T(128)} %bitcast.105, f32[]{:T(128)} %bitcast.106, ...), kind=kLoop, calls=%fused_computation.24.clone.1 | loop fusion | flops 4194304 | bytes 2097216 | tf_op jit(solution)/shard_map/while/body/eval_jaxpr/stack | solution.py:41
  506.7 10.0 %fusion.44 = (f32[256,512]{1,0:T(8,128)}, f32[256,512]{1,0:T(8,128)S(1)}) fusion(f32[]{:T(128)} %bitcast.105, f32[]{:T(128)} %bitcast.106, f32[]{:T(128)} %bitcast.113, f32[]{:T(128)} %bitcast.107, f32[]{:T(128)} %bitcast.108, f32[]{:T(128)} %bitcast.114, f32[]{:T(128)} %bitcast.109, f32[]{:T(128)} %bitcast.110, f32[]{:T(128)} %bitcast.115, ...), kind=kLoop, calls=%fused_computation.29.clone.1 | loop fusion | flops 3407872 | bytes 2097201 | tf_op jit(solution)/shard_map/while/body/eval_jaxpr/mul | solution.py:83
  521.3 12.2 %multiply_bitcast_fusion.5 = (f32[1,256,512]{2,1,0:T(8,128)S(1)}, f32[256,512]{1,0:T(8,128)S(1)}) fusion(f32[]{:T(128)} %bitcast.101, f32[]{:T(128)} %bitcast.102, f32[]{:T(128)} %bitcast.103, f32[]{:T(128)} %bitcast.104, f32[]{:T(128)} %bitcast.105, f32[]{:T(128)} %bitcast.106, f32[258,514]{1,0:T(8,128)S(1)} %bitcast_convert_fusion.2, f32[]{:T(128)} %bitcast.107, ...), kind=kLoop, calls=%fused_computation.25.clone.1 | loop fusion | flops 6815744 | bytes 4194372 | tf_op jit(solution)/shard_map/while/body/eval_jaxpr/stack | solution.py:41
  533.5 11.8 %multiply_bitcast_fusion.6 = (f32[1,256,512]{2,1,0:T(8,128)S(1)}, f32[1,256,512]{2,1,0:T(8,128)}) fusion(f32[256,512]{1,0:T(8,128)S(1)} %get-tuple-element.294, f32[]{:T(128)} %bitcast.117, f32[]{:T(128)} %bitcast.118, f32[]{:T(128)} %bitcast.119, f32[]{:T(128)} %bitcast.120, f32[]{:T(128)} %bitcast.105, f32[]{:T(128)} %bitcast.106, ...), kind=kLoop, calls=%fused_computation.24.clone.1 | loop fusion | flops 4194304 | bytes 2097216 | tf_op jit(solution)/shard_map/while/body/eval_jaxpr/stack | solution.py:41
  545.3 10.0 %fusion.44 = (f32[256,512]{1,0:T(8,128)}, f32[256,512]{1,0:T(8,128)S(1)}) fusion(f32[]{:T(128)} %bitcast.105, f32[]{:T(128)} %bitcast.106, f32[]{:T(128)} %bitcast.113, f32[]{:T(128)} %bitcast.107, f32[]{:T(128)} %bitcast.108, f32[]{:T(128)} %bitcast.114, f32[]{:T(128)} %bitcast.109, f32[]{:T(128)} %bitcast.110, f32[]{:T(128)} %bitcast.115, ...), kind=kLoop, calls=%fused_computation.29.clone.1 | loop fusion | flops 3407872 | bytes 2097201 | tf_op jit(solution)/shard_map/while/body/eval_jaxpr/mul | solution.py:83
  560.0 12.2 %multiply_bitcast_fusion.5 = (f32[1,256,512]{2,1,0:T(8,128)S(1)}, f32[256,512]{1,0:T(8,128)S(1)}) fusion(f32[]{:T(128)} %bitcast.101, f32[]{:T(128)} %bitcast.102, f32[]{:T(128)} %bitcast.103, f32[]{:T(128)} %bitcast.104, f32[]{:T(128)} %bitcast.105, f32[]{:T(128)} %bitcast.106, f32[258,514]{1,0:T(8,128)S(1)} %bitcast_convert_fusion.2, f32[]{:T(128)} %bitcast.107, ...), kind=kLoop, calls=%fused_computation.25.clone.1 | loop fusion | flops 6815744 | bytes 4194372 | tf_op jit(solution)/shard_map/while/body/eval_jaxpr/stack | solution.py:41
  572.2 11.8 %multiply_bitcast_fusion.6 = (f32[1,256,512]{2,1,0:T(8,128)S(1)}, f32[1,256,512]{2,1,0:T(8,128)}) fusion(f32[256,512]{1,0:T(8,128)S(1)} %get-tuple-element.294, f32[]{:T(128)} %bitcast.117, f32[]{:T(128)} %bitcast.118, f32[]{:T(128)} %bitcast.119, f32[]{:T(128)} %bitcast.120, f32[]{:T(128)} %bitcast.105, f32[]{:T(128)} %bitcast.106, ...), kind=kLoop, calls=%fused_computation.24.clone.1 | loop fusion | flops 4194304 | bytes 2097216 | tf_op jit(solution)/shard_map/while/body/eval_jaxpr/stack | solution.py:41
  583.9 10.0 %fusion.44 = (f32[256,512]{1,0:T(8,128)}, f32[256,512]{1,0:T(8,128)S(1)}) fusion(f32[]{:T(128)} %bitcast.105, f32[]{:T(128)} %bitcast.106, f32[]{:T(128)} %bitcast.113, f32[]{:T(128)} %bitcast.107, f32[]{:T(128)} %bitcast.108, f32[]{:T(128)} %bitcast.114, f32[]{:T(128)} %bitcast.109, f32[]{:T(128)} %bitcast.110, f32[]{:T(128)} %bitcast.115, ...), kind=kLoop, calls=%fused_computation.29.clone.1 | loop fusion | flops 3407872 | bytes 2097201 | tf_op jit(solution)/shard_map/while/body/eval_jaxpr/mul | solution.py:83
  598.6 12.2 %multiply_bitcast_fusion.5 = (f32[1,256,512]{2,1,0:T(8,128)S(1)}, f32[256,512]{1,0:T(8,128)S(1)}) fusion(f32[]{:T(128)} %bitcast.101, f32[]{:T(128)} %bitcast.102, f32[]{:T(128)} %bitcast.103, f32[]{:T(128)} %bitcast.104, f32[]{:T(128)} %bitcast.105, f32[]{:T(128)} %bitcast.106, f32[258,514]{1,0:T(8,128)S(1)} %bitcast_convert_fusion.2, f32[]{:T(128)} %bitcast.107, ...), kind=kLoop, calls=%fused_computation.25.clone.1 | loop fusion | flops 6815744 | bytes 4194372 | tf_op jit(solution)/shard_map/while/body/eval_jaxpr/stack | solution.py:41
  610.8 11.8 %multiply_bitcast_fusion.6 = (f32[1,256,512]{2,1,0:T(8,128)S(1)}, f32[1,256,512]{2,1,0:T(8,128)}) fusion(f32[256,512]{1,0:T(8,128)S(1)} %get-tuple-element.294, f32[]{:T(128)} %bitcast.117, f32[]{:T(128)} %bitcast.118, f32[]{:T(128)} %bitcast.119, f32[]{:T(128)} %bitcast.120, f32[]{:T(128)} %bitcast.105, f32[]{:T(128)} %bitcast.106, ...), kind=kLoop, calls=%fused_computation.24.clone.1 | loop fusion | flops 4194304 | bytes 2097216 | tf_op jit(solution)/shard_map/while/body/eval_jaxpr/stack | solution.py:41
  622.5 10.0 %fusion.44 = (f32[256,512]{1,0:T(8,128)}, f32[256,512]{1,0:T(8,128)S(1)}) fusion(f32[]{:T(128)} %bitcast.105, f32[]{:T(128)} %bitcast.106, f32[]{:T(128)} %bitcast.113, f32[]{:T(128)} %bitcast.107, f32[]{:T(128)} %bitcast.108, f32[]{:T(128)} %bitcast.114, f32[]{:T(128)} %bitcast.109, f32[]{:T(128)} %bitcast.110, f32[]{:T(128)} %bitcast.115, ...), kind=kLoop, calls=%fused_computation.29.clone.1 | loop fusion | flops 3407872 | bytes 2097201 | tf_op jit(solution)/shard_map/while/body/eval_jaxpr/mul | solution.py:83
  637.2 12.2 %multiply_bitcast_fusion.5 = (f32[1,256,512]{2,1,0:T(8,128)S(1)}, f32[256,512]{1,0:T(8,128)S(1)}) fusion(f32[]{:T(128)} %bitcast.101, f32[]{:T(128)} %bitcast.102, f32[]{:T(128)} %bitcast.103, f32[]{:T(128)} %bitcast.104, f32[]{:T(128)} %bitcast.105, f32[]{:T(128)} %bitcast.106, f32[258,514]{1,0:T(8,128)S(1)} %bitcast_convert_fusion.2, f32[]{:T(128)} %bitcast.107, ...), kind=kLoop, calls=%fused_computation.25.clone.1 | loop fusion | flops 6815744 | bytes 4194372 | tf_op jit(solution)/shard_map/while/body/eval_jaxpr/stack | solution.py:41
  649.4 11.8 %multiply_bitcast_fusion.6 = (f32[1,256,512]{2,1,0:T(8,128)S(1)}, f32[1,256,512]{2,1,0:T(8,128)}) fusion(f32[256,512]{1,0:T(8,128)S(1)} %get-tuple-element.294, f32[]{:T(128)} %bitcast.117, f32[]{:T(128)} %bitcast.118, f32[]{:T(128)} %bitcast.119, f32[]{:T(128)} %bitcast.120, f32[]{:T(128)} %bitcast.105, f32[]{:T(128)} %bitcast.106, ...), kind=kLoop, calls=%fused_computation.24.clone.1 | loop fusion | flops 4194304 | bytes 2097216 | tf_op jit(solution)/shard_map/while/body/eval_jaxpr/stack | solution.py:41
  661.1 10.0 %fusion.44 = (f32[256,512]{1,0:T(8,128)}, f32[256,512]{1,0:T(8,128)S(1)}) fusion(f32[]{:T(128)} %bitcast.105, f32[]{:T(128)} %bitcast.106, f32[]{:T(128)} %bitcast.113, f32[]{:T(128)} %bitcast.107, f32[]{:T(128)} %bitcast.108, f32[]{:T(128)} %bitcast.114, f32[]{:T(128)} %bitcast.109, f32[]{:T(128)} %bitcast.110, f32[]{:T(128)} %bitcast.115, ...), kind=kLoop, calls=%fused_computation.29.clone.1 | loop fusion | flops 3407872 | bytes 2097201 | tf_op jit(solution)/shard_map/while/body/eval_jaxpr/mul | solution.py:83
  673.8 2.4 collective-permute-start.6
  676.2 24.0 %collective-permute-done.6 = f32[4,4,32,512]{3,2,1,0:T(8,128)} collective-permute-done((f32[4,4,32,512]{3,2,1,0:T(8,128)S(1)}, f32[4,4,32,512]{3,2,1,0:T(8,128)}, u32[]{:S(2)}, u32[]{:S(2)}) %collective-permute-start.6) | collective-permute-done | bytes 1048608 | tf_op jit(solution)/shard_map/ppermute | solution.py:21
  700.2 1.6 broadcast_select_fusion.2
  702.2 1.6 collective-permute-start.7
  703.8 12.2 %collective-permute-done.7 = f32[4,2,32,512]{3,2,1,0:T(8,128)S(1)} collective-permute-done((f32[4,2,32,512]{3,2,1,0:T(8,128)S(1)}, f32[4,2,32,512]{3,2,1,0:T(8,128)S(1)}, u32[]{:S(2)}, u32[]{:S(2)}) %collective-permute-start.7) | collective-permute-done | bytes 524320 | tf_op jit(solution)/shard_map/ppermute | solution.py:21
  716.4 2.7 collective-permute-start.8
  719.0 11.3 %collective-permute-done.8 = f32[4,1,32,512]{3,2,1,0:T(8,128)S(1)} collective-permute-done((f32[4,1,32,512]{3,2,1,0:T(8,128)S(1)}, f32[4,1,32,512]{3,2,1,0:T(8,128)S(1)}, u32[]{:S(2)}, u32[]{:S(2)}) %collective-permute-start.8) | collective-permute-done | bytes 262176 | tf_op jit(solution)/shard_map/ppermute | solution.py:21
  (120 shorter events, 84.2 us)
Async XLA Ops:
  1.0 14.1 %collective-permute-start = (bf16[16,1,512]{2,0,1:T(8,128)(2,1)S(1)}, bf16[16,1,512]{2,0,1:T(8,128)(2,1)S(1)}, u32[]{:S(2)}, u32[]{:S(2)}) collective-permute-start(bf16[16,1,512]{2,0,1:T(8,128)(2,1)S(1)} %copy.23), channel_id=1, source_target_pairs={{0,2},{1,3},{4,6},{5,7},{8,10},{9,11},{12,14},{13,15},{16,18},{17,... | collective-permute-start | bytes 49160 | tf_op jit(solution)/shard_map/ppermute | solution.py:12
  5.9 11.3 %collective-permute-start.1 = (bf16[16,1,512]{2,0,1:T(8,128)(2,1)S(1)}, bf16[16,1,512]{2,0,1:T(8,128)(2,1)S(1)}, u32[]{:S(2)}, u32[]{:S(2)}) collective-permute-start(bf16[16,1,512]{2,0,1:T(8,128)(2,1)S(1)} %copy.24), channel_id=1, source_target_pairs={{2,0},{3,1},{6,4},{7,5},{10,8},{11,9},{14,12},{15,13},{18,16},{19,... | collective-permute-start | bytes 49160 | tf_op jit(solution)/shard_map/ppermute | solution.py:15
  17.2 3.8 copy-start
  21.0 9.8 %collective-permute-start.2 = (bf16[16,258,1]{1,0,2:T(8,128)(2,1)S(1)}, bf16[16,258,1]{1,0,2:T(8,128)(2,1)S(1)}, u32[]{:S(2)}, u32[]{:S(2)}) collective-permute-start(bf16[16,258,1]{1,0,2:T(8,128)(2,1)S(1)} %get-tuple-element.167), channel_id=1, source_target_pairs={{0,1},{2,3},{4,5},{6,7},{8,9},{10,11},{12,13},{14,15},{16,17},{18,... | collective-permute-start | bytes 24776 | tf_op jit(solution)/shard_map/ppermute | solution.py:12
  22.5 8.3 %collective-permute-start.3 = (bf16[16,258,1]{1,0,2:T(8,128)(2,1)S(1)}, bf16[16,258,1]{1,0,2:T(8,128)(2,1)S(1)}, u32[]{:S(2)}, u32[]{:S(2)}) collective-permute-start(bf16[16,258,1]{1,0,2:T(8,128)(2,1)S(1)} %get-tuple-element.168), channel_id=1, source_target_pairs={{1,0},{3,2},{5,4},{7,6},{9,8},{11,10},{13,12},{15,14},{17,16},{19,... | collective-permute-start | bytes 24776 | tf_op jit(solution)/shard_map/ppermute | solution.py:15
  24.8 25.2 %collective-permute-start.4 = (bf16[1,256,512]{2,1,0:T(8,128)(2,1)S(1)}, bf16[1,256,512]{2,1,0:T(8,128)(2,1)S(1)}, u32[]{:S(2)}, u32[]{:S(2)}) collective-permute-start(bf16[1,256,512]{2,1,0:T(8,128)(2,1)S(1)} %get-tuple-element.172), channel_id=1, source_target_pairs={{4,0},{8,4},{12,8},{16,12},{20,16},{24,20},{28,24},{5,1},{9,5},{13... | collective-permute-start | bytes 786440 | tf_op jit(solution)/shard_map/ppermute | solution.py:15
  26.1 23.9 %collective-permute-start.5 = (bf16[1,256,512]{2,1,0:T(8,128)(2,1)S(1)}, bf16[1,256,512]{2,1,0:T(8,128)(2,1)S(1)}, u32[]{:S(2)}, u32[]{:S(2)}) collective-permute-start(bf16[1,256,512]{2,1,0:T(8,128)(2,1)S(1)} %get-tuple-element.171), channel_id=1, source_target_pairs={{0,4},{4,8},{8,12},{12,16},{16,20},{20,24},{24,28},{1,5},{5,9},{9,... | collective-permute-start | bytes 786440 | tf_op jit(solution)/shard_map/ppermute | solution.py:12
  50.0 5.9 copy-start.1
  50.0 5.9 copy-start.2
  50.0 5.9 copy-start.3
  50.0 5.9 copy-start.4
  673.8 26.4 %collective-permute-start.6 = (f32[4,4,32,512]{3,2,1,0:T(8,128)S(1)}, f32[4,4,32,512]{3,2,1,0:T(8,128)}, u32[]{:S(2)}, u32[]{:S(2)}) collective-permute-start(f32[4,4,32,512]{3,2,1,0:T(8,128)S(1)} %fusion.18), channel_id=1, source_target_pairs={{0,4},{4,0},{8,12},{12,8},{16,20},{20,16},{24,28},{28,24},{1,5},{5... | collective-permute-start | bytes 3145736 | tf_op jit(solution)/shard_map/ppermute | solution.py:21
  702.2 13.9 %collective-permute-start.7 = (f32[4,2,32,512]{3,2,1,0:T(8,128)S(1)}, f32[4,2,32,512]{3,2,1,0:T(8,128)S(1)}, u32[]{:S(2)}, u32[]{:S(2)}) collective-permute-start(f32[4,2,32,512]{3,2,1,0:T(8,128)S(1)} %dynamic-slice_bitcast_fusion), channel_id=1, source_target_pairs={{0,8},{4,12},{8,0},{12,4},{16,24},{20,28},{24,16},{28,20},{1,9},{5... | collective-permute-start | bytes 1572872 | tf_op jit(solution)/shard_map/ppermute | solution.py:21
  716.4 13.9 %collective-permute-start.8 = (f32[4,1,32,512]{3,2,1,0:T(8,128)S(1)}, f32[4,1,32,512]{3,2,1,0:T(8,128)S(1)}, u32[]{:S(2)}, u32[]{:S(2)}) collective-permute-start(f32[4,1,32,512]{3,2,1,0:T(8,128)S(1)} %fusion.23), channel_id=1, source_target_pairs={{0,16},{4,20},{8,24},{12,28},{16,0},{20,4},{24,8},{28,12},{1,17},{... | collective-permute-start | bytes 786440 | tf_op jit(solution)/shard_map/ppermute | solution.py:21
where the time goes:
time: 741 us; the launch traced here: 731 us
  other arithmetic  604 us (82%)
  local copies, waits for them, and re-layouts  57.4 us (8%)
  waiting for transfers between devices  47.5 us (6%)
  starting transfers between devices  21.5 us (3%)
    another operation x32, other arithmetic, shading(): glowing = jnp.stack([emitted * weight for emitted in emission])  383 us
    mul x16, other arithmetic, march_layer(): return ((color_sum + passed[None] * glowing, passed * passing), None)  160 us
    ppermute x3, waiting for transfers between devices, partner(): lax.ppermute(array, axis, [(i, i ^ 1 << distance) for i in range(lax.axis...  47.5 us
    add x16, other arithmetic, march_layer(): return ((color_sum + passed[None] * glowing, passed * passing), None)  24.3 us
    unnamed x14, local copies, waits for them, and re-layouts  17.5 us
    convert_element_type x16, other arithmetic, march_layer(): side = side.astype(jnp.float32)  16.3 us
    concatenate x2, other arithmetic, extended(): block = jnp.concatenate([low, block, high], axis=dim)  15.6 us
  transfers between devices with their start and end apart: 9, of which 3 were waited for; matrix products, arithmetic and copies ran while one was open for 4% of the time, Pallas kernels for 0%

commit v1 on v0

v1 whole, which is shorter than its diff:
```python
import functools
import math

import jax
import jax.numpy as jnp
from jax import lax
from jax.experimental import pallas as pl
from jax.experimental.pallas import tpu as pltpu
from jax.sharding import PartitionSpec as P

LOG2E = math.log2(math.e)
RS = 16
CS = 128
CH = 32


def fill_bands(dcol, drow):
    k = lax.broadcasted_iota(jnp.int32, dcol.shape, 0)
    j = lax.broadcasted_iota(jnp.int32, dcol.shape, 1)
    dcol[...] = jnp.where(k == j + CS + 1, 1.0, jnp.where(k == j + CS - 1, -1.0, 0.0)).astype(dcol.dtype)
    i = lax.broadcasted_iota(jnp.int32, drow.shape, 0)
    k = lax.broadcasted_iota(jnp.int32, drow.shape, 1)
    drow[...] = jnp.where(k == i + RS + 1, 1.0, jnp.where(k == i + RS - 1, -1.0, 0.0)).astype(drow.dtype)


def tables(layers_all, centers, widths, colors, opacity):
    scale = 1.5 / layers_all * LOG2E
    cen, quad, off = [], [], []
    mat = [[], [], []]
    for k in range(4):
        w = jnp.full((8, 128), widths[k], jnp.float32)
        o = jnp.full((8, 128), opacity[k], jnp.float32) * scale
        cen.append(jnp.full((8, 128), centers[k], jnp.float32))
        quad.append(-LOG2E / (w * w))
        off.append(jnp.log2(o))
        for c in range(3):
            mat[c].append(0.7 * colors[c, k] / o)
    return cen, quad, off, mat


def march_chunk(r0, ext, cscr, rscr, dcol, drow, tab, store):
    layers = ext.shape[0] - 2
    cols = ext.shape[2] - 2 * CS
    for h in range(cols // 256):
        left = ext[1 : layers + 1, pl.ds(r0 + RS, CH), h * 256 : h * 256 + 512].reshape(layers * CH, 512)
        cscr[:, :, h * 256 : h * 256 + 256] = jnp.dot(
            left, dcol[...], preferred_element_type=jnp.float32
        ).reshape(layers, CH, 256)
    for z in range(layers):
        rscr[z] = jnp.dot(
            drow[...], ext[1 + z, pl.ds(r0, CH + 2 * RS), CS : CS + cols], preferred_element_type=jnp.float32
        )
    cen8, quad8, off8, mat8 = tab
    two = lambda v: jnp.concatenate([v, v], axis=0)
    tiles = cols // 128

    def tile(t, _):
        q0 = pl.multiple_of(t // tiles * 16, 16)
        l0 = pl.multiple_of(t % tiles * 128, 128)
        cen, quad, off = [two(v) for v in cen8], [two(v) for v in quad8], [two(v) for v in off8]
        plane = lambda z: ext[z, pl.ds(pl.multiple_of(r0 + q0 + RS, 16), 16), pl.ds(l0 + CS, 128)].astype(jnp.float32)
        acc = [jnp.zeros((16, 128), jnp.float32) for _ in range(4)]
        expo = jnp.zeros((16, 128), jnp.float32)
        passed = jnp.ones((16, 128), jnp.float32)
        before, s = plane(0), plane(1)
        for z in range(layers):
            after = plane(z + 2)
            d = after - before
            r = rscr[z, pl.ds(q0, 16), pl.ds(l0, 128)]
            c = cscr[z, pl.ds(q0, 16), pl.ds(l0, 128)]
            light = jnp.abs(d) * lax.rsqrt(d * d + r * r + (c * c + 1.0)) + (0.3 / 0.7)
            bump = []
            for k in range(4):
                u = s - cen[k]
                bump.append(jnp.exp2(u * u * quad[k] + off[k]))
            expo = expo - ((bump[0] + bump[1]) + (bump[2] + bump[3]))
            later = jnp.exp2(expo)
            weight = (passed - later) * light
            for k in range(4):
                acc[k] = acc[k] + weight * bump[k]
            passed = later
            before, s = s, after
        for ch in range(3):
            m = [two(v) for v in mat8[ch]]
            store(ch, q0, l0, (m[0] * acc[0] + m[1] * acc[1]) + (m[2] * acc[2] + m[3] * acc[3]))
        store(3, q0, l0, passed)
        return 0

    lax.fori_loop(0, CH // 16 * tiles, tile, 0)


def kernel(layers_all, vol, front, back, up, down, left, right, cen, wid, col, opa, out,
           ext, cscr, rscr, dcol, drow, sem):
    layers, rows, cols = vol.shape
    mid = (pl.ds(1, layers), pl.ds(RS, rows), pl.ds(CS, cols))
    pairs = [
        (vol, ext.at[mid]),
        (front, ext.at[pl.ds(0, 1), mid[1], mid[2]]),
        (back, ext.at[pl.ds(layers + 1, 1), mid[1], mid[2]]),
        (up, ext.at[mid[0], pl.ds(0, RS), mid[2]]),
        (down, ext.at[mid[0], pl.ds(RS + rows, RS), mid[2]]),
        (left, ext.at[mid[0], mid[1], pl.ds(0, CS)]),
        (right, ext.at[mid[0], mid[1], pl.ds(CS + cols, CS)]),
    ]
    copies = [pltpu.make_async_copy(a, b, sem.at[i]) for i, (a, b) in enumerate(pairs)]
    for c in copies:
        c.start()
    fill_bands(dcol, drow)
    tab = tables(layers_all, cen, wid, col, opa)
    for c in copies:
        c.wait()

    def chunk(j, _):
        r0 = pl.multiple_of(j * CH, CH)

        def store(ch, q0, l0, value):
            out[ch, pl.ds(pl.multiple_of(r0 + q0, 16), 16), pl.ds(l0, 128)] = value

        march_chunk(r0, ext, cscr, rscr, dcol, drow, tab, store)
        return 0

    lax.fori_loop(0, rows // CH, chunk, 0)


def shifted(block, axis, up):
    n = lax.axis_size(axis)
    pairs = [(i, i + 1) for i in range(n - 1)] if up else [(i + 1, i) for i in range(n - 1)]
    return lax.ppermute(block, axis, pairs)


def local(volume, cen, wid, col, opa):
    slabs = lax.axis_size("depth")
    me = lax.axis_index("depth")
    layers, rows, cols = volume.shape
    front = shifted(volume[-1:], "depth", True)
    back = shifted(volume[:1], "depth", False)
    up = shifted(volume[:, -RS:], "imgy", True)
    down = shifted(volume[:, :RS], "imgy", False)
    left = shifted(volume[:, :, -CS:], "imgx", True)
    right = shifted(volume[:, :, :CS], "imgx", False)
    hbm = pl.BlockSpec(memory_space=pl.ANY)
    smem = pl.BlockSpec(memory_space=pltpu.SMEM)
    part = pl.pallas_call(
        functools.partial(kernel, layers * slabs),
        out_shape=jax.ShapeDtypeStruct((4, rows, cols), jnp.float32),
        in_specs=[hbm] * 7 + [smem] * 4,
        out_specs=pl.BlockSpec(memory_space=pltpu.VMEM),
        scratch_shapes=[
            pltpu.VMEM((layers + 2, rows + 2 * RS, cols + 2 * CS), jnp.bfloat16),
            pltpu.VMEM((layers, CH, cols), jnp.float32),
            pltpu.VMEM((layers, CH, cols), jnp.float32),
            pltpu.VMEM((512, 256), jnp.bfloat16),
            pltpu.VMEM((CH, CH + 2 * RS), jnp.bfloat16),
            pltpu.SemaphoreType.DMA((7,)),
        ],
        compiler_params=pltpu.CompilerParams(vmem_limit_bytes=48 * 2**20),
        name="march",
    )(volume, front, back, up, down, left, right, cen, wid, col, opa)
    piece = rows // slabs
    for bit in range(slabs.bit_length() - 1):
        left_pieces = part.shape[1] // piece
        grouped = part.reshape(4, left_pieces // 2, 2, piece, cols)
        own = me // 2**bit % 2
        kept = lax.dynamic_index_in_dim(grouped, own, 2, keepdims=False)
        sent = lax.dynamic_index_in_dim(grouped, 1 - own, 2, keepdims=False)
        got = lax.ppermute(sent, "depth", [(i, i ^ 1 << bit) for i in range(slabs)])
        near = jnp.where(own == 0, kept, got)
        far = jnp.where(own == 0, got, kept)
        part = jnp.concatenate([near[:3] + near[3:] * far[:3], near[3:] * far[3:]], axis=0)
        part = part.reshape(4, left_pieces // 2 * piece, cols)
    return jnp.concatenate([part[:3], 1.0 - part[3:]], axis=0)[:, None]


def solution(mesh):
    return jax.shard_map(
        local,
        mesh=mesh,
        in_specs=(P("depth", "imgy", "imgx"), P(), P(), P(), P()),
        out_specs=P(None, "imgy", "depth", "imgx"),
        check_vma=False,
    )
```

time: 741 us -> 117 us (0.16); the launches traced: 731 us -> 117 us
  other arithmetic: 604 us -> 1.66 us
  local copies, waits for them, and re-layouts: 57.4 us -> 14.4 us
  Pallas kernels: 0 us -> 22.8 us
  waiting for transfers between devices: 47.5 us -> 57 us
    another operation x32 -> x0, other arithmetic: 383 us -> none  [shading(): glowing = jnp.stack([emitted * weight for emitted in emission])]
    mul x19 -> x3, other arithmetic: 160 us -> 0.07 us  [the longest x2 0.05 us: local(): near[3:] * far[:3]]
    slice x50 -> x3, local copies, waits for them, and re-layouts: 34.8 us -> 6.12 us  [the longest x1 3.18 us: local(): right = shifted(volume[:, :, :CS], 'imgx', False)]
    add x18 -> x2, other arithmetic: 24.6 us -> 0.27 us  [local(): near[:3] + near[3:] * far[:3]]
    pallas_call x0 -> x1, Pallas kernels: none -> 22.8 us  [local(): pl.pallas_call(functools.partial(kernel, layers * slabs), out_shape=jax.S...]
    convert_element_type x16 -> x0, other arithmetic: 16.3 us -> none  [march_layer(): side = side.astype(jnp.float32)]
    concatenate x4 -> x2, other arithmetic: 15.7 us -> 0.11 us  [local(): jnp.concatenate([near[:3] + near[3:] * far[:3], near[3:] * far[3:]], axis=0)]
    unnamed x14 -> x24, local copies, waits for them, and re-layouts: 17.5 us -> 7.17 us
  transfers between devices with their start and end apart: 9 -> 9, of which waited for: 3 -> 5; matrix products, arithmetic and copies ran while one was open for 4% -> 3% of each run, Pallas kernels for 0% -> 0%
where the time goes in v1:
time: 117 us
  waiting for transfers between devices  57 us (49%)
  Pallas kernels  22.8 us (19%)
  starting transfers between devices  20.5 us (18%)
  local copies, waits for them, and re-layouts  14.4 us (12%)
  other arithmetic  1.66 us (1%)
    ppermute x3, waiting for transfers between devices, local(): got = lax.ppermute(sent, 'depth', [(i, i ^ 1 << bit) for i in range(slabs)])  43.6 us
    pallas_call x1, Pallas kernels, local(): pl.pallas_call(functools.partial(kernel, layers * slabs), out_shape=jax.S...  22.8 us
    ppermute x6, starting transfers between devices, shifted(): return lax.ppermute(block, axis, pairs)  13.9 us
    ppermute x6, waiting for transfers between devices, shifted(): return lax.ppermute(block, axis, pairs)  13.4 us
    unnamed x24, local copies, waits for them, and re-layouts  7.17 us
    ppermute x3, starting transfers between devices, local(): got = lax.ppermute(sent, 'depth', [(i, i ^ 1 << bit) for i in range(slabs)])  6.55 us
    slice x1, local copies, waits for them, and re-layouts, local(): right = shifted(volume[:, :, :CS], 'imgx', False)  3.18 us
  transfers between devices with their start and end apart: 9, of which 5 were waited for; matrix products, arithmetic and copies ran while one was open for 3% of the time, Pallas kernels for 0%

profile of v1, /device:TPU:0, one launch (start us, length us, event | category | flops | bytes accessed | tf_op | source)
XLA Modules:
  0.0 116.6 jit_solution(2851846465562006581)
XLA Ops:
  0.0 0.0 copy-start.9
  0.0 0.0 copy-start.10
  0.0 0.0 copy-start.8
  0.0 0.0 copy-start.11
  0.0 3.2 %fusion.8 = (bf16[16,256,128]{2,1,0:T(8,128)(2,1)}, bf16[16,256,128]{2,1,0:T(8,128)(2,1)}) fusion(bf16[16,256,512]{2,1,0:T(8,128)(2,1)} %vol.1), kind=kLoop, calls=%fused_computation.31 | loop fusion | bytes 4194304 | tf_op jit(solution)/shard_map/slice | solution.py:140
  3.2 2.4 %collective-permute-start.4 = (bf16[16,256,128]{2,1,0:T(8,128)(2,1)}, bf16[16,256,128]{2,1,0:T(8,128)(2,1)S(1)}, u32[]{:S(2)}, u32[]{:S(2)}) collective-permute-start(bf16[16,256,128]{2,1,0:T(8,128)(2,1)} %get-tuple-element.6), channel_id=1, source_target_pairs={{0,1},{2,3},{4,5},{6,7},{8,9},{10,11},{12,13},{14,15},{16,17},{18,... | collective-permute-start | bytes 3145736 | tf_op jit(solution)/shard_map/ppermute | solution.py:128
  5.6 1.3 %collective-permute-start.5 = (bf16[16,256,128]{2,1,0:T(8,128)(2,1)}, bf16[16,256,128]{2,1,0:T(8,128)(2,1)S(1)}, u32[]{:S(2)}, u32[]{:S(2)}) collective-permute-start(bf16[16,256,128]{2,1,0:T(8,128)(2,1)} %get-tuple-element.5), channel_id=1, source_target_pairs={{1,0},{3,2},{5,4},{7,6},{9,8},{11,10},{13,12},{15,14},{17,16},{19,... | collective-permute-start | bytes 3145736 | tf_op jit(solution)/shard_map/ppermute | solution.py:128
  6.9 1.1 fusion.10
  8.0 4.2 %collective-permute-start = (bf16[1,256,512]{2,1,0:T(8,128)(2,1)S(1)}, bf16[1,256,512]{2,1,0:T(8,128)(2,1)S(1)}, u32[]{:S(2)}, u32[]{:S(2)}) collective-permute-start(bf16[1,256,512]{2,1,0:T(8,128)(2,1)S(1)} %get-tuple-element.10), channel_id=1, source_target_pairs={{0,4},{4,8},{8,12},{12,16},{16,20},{20,24},{24,28},{1,5},{5,9},{9,... | collective-permute-start | bytes 786440 | tf_op jit(solution)/shard_map/ppermute | solution.py:128
  12.2 1.3 %collective-permute-start.1 = (bf16[1,256,512]{2,1,0:T(8,128)(2,1)S(1)}, bf16[1,256,512]{2,1,0:T(8,128)(2,1)S(1)}, u32[]{:S(2)}, u32[]{:S(2)}) collective-permute-start(bf16[1,256,512]{2,1,0:T(8,128)(2,1)S(1)} %get-tuple-element.9), channel_id=1, source_target_pairs={{4,0},{8,4},{12,8},{16,12},{20,16},{24,20},{28,24},{5,1},{9,5},{13... | collective-permute-start | bytes 786440 | tf_op jit(solution)/shard_map/ppermute | solution.py:128
  13.5 1.9 %fusion.9 = (bf16[16,16,512]{2,1,0:T(8,128)(2,1)}, bf16[16,16,512]{2,1,0:T(8,128)(2,1)}) fusion(bf16[16,256,512]{2,1,0:T(8,128)(2,1)} %vol.1), kind=kLoop, calls=%fused_computation.32 | loop fusion | bytes 1048576 | tf_op jit(solution)/shard_map/slice | solution.py:138
  15.4 3.4 %collective-permute-start.2 = (bf16[16,16,512]{2,1,0:T(8,128)(2,1)}, bf16[16,16,512]{2,1,0:T(8,128)(2,1)S(1)}, u32[]{:S(2)}, u32[]{:S(2)}) collective-permute-start(bf16[16,16,512]{2,1,0:T(8,128)(2,1)} %get-tuple-element.8), channel_id=1, source_target_pairs={{0,2},{1,3},{4,6},{5,7},{8,10},{9,11},{12,14},{13,15},{16,18},{17,... | collective-permute-start | bytes 786440 | tf_op jit(solution)/shard_map/ppermute | solution.py:128
  18.8 5.4 %collective-permute-done.front = bf16[1,256,512]{2,1,0:T(8,128)(2,1)S(1)} collective-permute-done((bf16[1,256,512]{2,1,0:T(8,128)(2,1)S(1)}, bf16[1,256,512]{2,1,0:T(8,128)(2,1)S(1)}, u32[]{:S(2)}, u32[]{:S(2)}) %collective-permute-start) | collective-permute-done | bytes 262176 | tf_op jit(solution)/shard_map/ppermute | solution.py:128
  24.3 1.3 %collective-permute-start.3 = (bf16[16,16,512]{2,1,0:T(8,128)(2,1)}, bf16[16,16,512]{2,1,0:T(8,128)(2,1)S(1)}, u32[]{:S(2)}, u32[]{:S(2)}) collective-permute-start(bf16[16,16,512]{2,1,0:T(8,128)(2,1)} %get-tuple-element.7), channel_id=1, source_target_pairs={{2,0},{3,1},{6,4},{7,5},{10,8},{11,9},{14,12},{15,13},{18,16},{19,... | collective-permute-start | bytes 786440 | tf_op jit(solution)/shard_map/ppermute | solution.py:128
  25.6 0.0 collective-permute-done.1.back
  25.6 0.0 copy-start.2
  25.6 0.7 copy-done.2
  26.3 0.0 collective-permute-done.2.up
  26.3 0.0 copy-start.4
  26.3 0.7 copy-done.4
  27.0 7.9 %collective-permute-done.3.down = bf16[16,16,512]{2,1,0:T(8,128)(2,1)S(1)} collective-permute-done((bf16[16,16,512]{2,1,0:T(8,128)(2,1)}, bf16[16,16,512]{2,1,0:T(8,128)(2,1)S(1)}, u32[]{:S(2)}, u32[]{:S(2)}) %collective-permute-start.3) | collective-permute-done | bytes 262176 | tf_op jit(solution)/shard_map/ppermute | solution.py:128
  34.9 0.0 copy-start.6
  34.9 0.7 copy-done.6
  35.6 0.0 collective-permute-done.4.left
  35.6 0.0 collective-permute-done.5.right
  35.6 0.0 copy-start
  35.6 1.0 copy-done
  36.6 0.0 copy-done.9
  36.6 0.0 copy-done.10
  36.6 0.0 copy-done.8
  36.6 0.0 copy-done.11
  36.6 0.0 copy-start.1
  36.7 1.2 %copy-done.1 = bf16[16,256,128]{2,1,0:T(8,128)(2,1)S(1)} copy-done((bf16[16,256,128]{2,1,0:T(8,128)(2,1)S(1)}, bf16[16,256,128]{2,1,0:T(8,128)(2,1)}, u32[]{:S(2)}) %copy-start.1) | copy-done | bytes 1048600
  37.9 0.0 copy-start.3
  37.9 0.9 copy-done.3
  38.8 0.0 copy-start.5
  38.8 0.9 copy-done.5
  39.8 0.0 copy-start.7
  39.8 0.9 copy-done.7
  40.7 22.8 %march.1 = f32[4,256,512]{2,1,0:T(8,128)S(1)} custom-call(bf16[16,256,512]{2,1,0:T(8,128)(2,1)} %vol.1, bf16[1,256,512]{2,1,0:T(8,128)(2,1)S(1)} %collective-permute-done.front, bf16[1,256,512]{2,1,0:T(8,128)(2,1)S(1)} %copy-done.3, bf16[16,16,512]{2,1,0:T(8,128)(2,1)S(1)} %copy-done.5, bf16[16,16,512]{2,1,0:T(8,128)(2,1)S(1)} %copy-done.7, ...), custom_call_target="tpu_custom_call" | custom-call | tf_op jit(solution)/shard_map/march/pallas_call | solution.py:143
  63.6 1.1 dynamic-slice_bitcast_fusion
  64.7 2.3 %collective-permute-start.6 = (f32[4,4,32,512]{3,2,1,0:T(8,128)}, f32[4,4,32,512]{3,2,1,0:T(8,128)S(1)}, u32[]{:S(2)}, u32[]{:S(2)}) collective-permute-start(f32[4,4,32,512]{3,2,1,0:T(8,128)} %dynamic-slice_bitcast_fusion), channel_id=1, source_target_pairs={{0,4},{4,0},{8,12},{12,8},{16,20},{20,16},{24,28},{28,24},{1,5},{5... | collective-permute-start | bytes 3145736 | tf_op jit(solution)/shard_map/ppermute | solution.py:166
  66.9 22.8 %collective-permute-done.6 = f32[4,4,32,512]{3,2,1,0:T(8,128)S(1)} collective-permute-done((f32[4,4,32,512]{3,2,1,0:T(8,128)}, f32[4,4,32,512]{3,2,1,0:T(8,128)S(1)}, u32[]{:S(2)}, u32[]{:S(2)}) %collective-permute-start.6) | collective-permute-done | bytes 1048608 | tf_op jit(solution)/shard_map/ppermute | solution.py:166
  89.7 0.2 bitcast_select_fusion.1
  90.0 0.2 fusion
  90.2 0.1 pad_maximum_fusion
  90.4 1.6 %collective-permute-start.7 = (f32[4,2,32,512]{3,2,1,0:T(8,128)S(1)}, f32[4,2,32,512]{3,2,1,0:T(8,128)S(1)}, u32[]{:S(2)}, u32[]{:S(2)}) collective-permute-start(f32[4,2,32,512]{3,2,1,0:T(8,128)S(1)} %dynamic-slice_bitcast_fusion.1), channel_id=1, source_target_pairs={{0,8},{4,12},{8,0},{12,4},{16,24},{20,28},{24,16},{28,20},{1,9},{5... | collective-permute-start | bytes 1572872 | tf_op jit(solution)/shard_map/ppermute | solution.py:166
  92.0 10.9 %collective-permute-done.7 = f32[4,2,32,512]{3,2,1,0:T(8,128)S(1)} collective-permute-done((f32[4,2,32,512]{3,2,1,0:T(8,128)S(1)}, f32[4,2,32,512]{3,2,1,0:T(8,128)S(1)}, u32[]{:S(2)}, u32[]{:S(2)}) %collective-permute-start.7) | collective-permute-done | bytes 524320 | tf_op jit(solution)/shard_map/ppermute | solution.py:166
  102.9 0.2 bitcast_select_fusion.3
  103.1 0.1 fusion.1
  103.2 2.7 %collective-permute-start.8 = (f32[4,1,32,512]{3,2,1,0:T(8,128)S(1)}, f32[4,1,32,512]{3,2,1,0:T(8,128)S(1)}, u32[]{:S(2)}, u32[]{:S(2)}) collective-permute-start(f32[4,1,32,512]{3,2,1,0:T(8,128)S(1)} %fusion.2), channel_id=1, source_target_pairs={{0,16},{4,20},{8,24},{12,28},{16,0},{20,4},{24,8},{28,12},{1,17},{... | collective-permute-start | bytes 786440 | tf_op jit(solution)/shard_map/ppermute | solution.py:166
  105.9 9.9 %collective-permute-done.8 = f32[4,1,32,512]{3,2,1,0:T(8,128)S(1)} collective-permute-done((f32[4,1,32,512]{3,2,1,0:T(8,128)S(1)}, f32[4,1,32,512]{3,2,1,0:T(8,128)S(1)}, u32[]{:S(2)}, u32[]{:S(2)}) %collective-permute-start.8) | collective-permute-done | bytes 262176 | tf_op jit(solution)/shard_map/ppermute | solution.py:166
  115.8 0.1 broadcast_select_fusion.1
  115.9 0.7 maximum_bitcast_fusion
  (6 shorter events, 0.2 us)
Async XLA Ops:
  0.0 36.6 %copy-start.9 = (f32[4]{0:T(128)S(1)}, f32[4]{0:T(128)}, u32[]{:S(2)}) copy-start(f32[4]{0:T(128)} %cen.1) | copy-start | bytes 52
  0.0 36.6 %copy-start.10 = (f32[4]{0:T(128)S(1)}, f32[4]{0:T(128)}, u32[]{:S(2)}) copy-start(f32[4]{0:T(128)} %wid.1) | copy-start | bytes 52
  0.0 36.6 %copy-start.8 = (f32[3,4]{1,0:T(4,128)S(1)}, f32[3,4]{1,0:T(4,128)}, u32[]{:S(2)}) copy-start(f32[3,4]{1,0:T(4,128)} %col.1) | copy-start | bytes 148
  0.0 36.6 %copy-start.11 = (f32[4]{0:T(128)S(1)}, f32[4]{0:T(128)}, u32[]{:S(2)}) copy-start(f32[4]{0:T(128)} %opa.1) | copy-start | bytes 52
  3.2 32.5 %collective-permute-start.4 = (bf16[16,256,128]{2,1,0:T(8,128)(2,1)}, bf16[16,256,128]{2,1,0:T(8,128)(2,1)S(1)}, u32[]{:S(2)}, u32[]{:S(2)}) collective-permute-start(bf16[16,256,128]{2,1,0:T(8,128)(2,1)} %get-tuple-element.6), channel_id=1, source_target_pairs={{0,1},{2,3},{4,5},{6,7},{8,9},{10,11},{12,13},{14,15},{16,17},{18,... | collective-permute-start | bytes 3145736 | tf_op jit(solution)/shard_map/ppermute | solution.py:128
  5.6 30.0 %collective-permute-start.5 = (bf16[16,256,128]{2,1,0:T(8,128)(2,1)}, bf16[16,256,128]{2,1,0:T(8,128)(2,1)S(1)}, u32[]{:S(2)}, u32[]{:S(2)}) collective-permute-start(bf16[16,256,128]{2,1,0:T(8,128)(2,1)} %get-tuple-element.5), channel_id=1, source_target_pairs={{1,0},{3,2},{5,4},{7,6},{9,8},{11,10},{13,12},{15,14},{17,16},{19,... | collective-permute-start | bytes 3145736 | tf_op jit(solution)/shard_map/ppermute | solution.py:128
  8.0 16.3 %collective-permute-start = (bf16[1,256,512]{2,1,0:T(8,128)(2,1)S(1)}, bf16[1,256,512]{2,1,0:T(8,128)(2,1)S(1)}, u32[]{:S(2)}, u32[]{:S(2)}) collective-permute-start(bf16[1,256,512]{2,1,0:T(8,128)(2,1)S(1)} %get-tuple-element.10), channel_id=1, source_target_pairs={{0,4},{4,8},{8,12},{12,16},{16,20},{20,24},{24,28},{1,5},{5,9},{9,... | collective-permute-start | bytes 786440 | tf_op jit(solution)/shard_map/ppermute | solution.py:128
  12.2 13.4 %collective-permute-start.1 = (bf16[1,256,512]{2,1,0:T(8,128)(2,1)S(1)}, bf16[1,256,512]{2,1,0:T(8,128)(2,1)S(1)}, u32[]{:S(2)}, u32[]{:S(2)}) collective-permute-start(bf16[1,256,512]{2,1,0:T(8,128)(2,1)S(1)} %get-tuple-element.9), channel_id=1, source_target_pairs={{4,0},{8,4},{12,8},{16,12},{20,16},{24,20},{28,24},{5,1},{9,5},{13... | collective-permute-start | bytes 786440 | tf_op jit(solution)/shard_map/ppermute | solution.py:128
  15.4 10.9 %collective-permute-start.2 = (bf16[16,16,512]{2,1,0:T(8,128)(2,1)}, bf16[16,16,512]{2,1,0:T(8,128)(2,1)S(1)}, u32[]{:S(2)}, u32[]{:S(2)}) collective-permute-start(bf16[16,16,512]{2,1,0:T(8,128)(2,1)} %get-tuple-element.8), channel_id=1, source_target_pairs={{0,2},{1,3},{4,6},{5,7},{8,10},{9,11},{12,14},{13,15},{16,18},{17,... | collective-permute-start | bytes 786440 | tf_op jit(solution)/shard_map/ppermute | solution.py:128
  24.3 10.6 %collective-permute-start.3 = (bf16[16,16,512]{2,1,0:T(8,128)(2,1)}, bf16[16,16,512]{2,1,0:T(8,128)(2,1)S(1)}, u32[]{:S(2)}, u32[]{:S(2)}) collective-permute-start(bf16[16,16,512]{2,1,0:T(8,128)(2,1)} %get-tuple-element.7), channel_id=1, source_target_pairs={{2,0},{3,1},{6,4},{7,5},{10,8},{11,9},{14,12},{15,13},{18,16},{19,... | collective-permute-start | bytes 786440 | tf_op jit(solution)/shard_map/ppermute | solution.py:128
  25.6 0.7 copy-start.2
  26.3 0.7 copy-start.4
  34.9 0.7 copy-start.6
  35.6 1.0 copy-start
  36.6 1.2 %copy-start.1 = (bf16[16,256,128]{2,1,0:T(8,128)(2,1)S(1)}, bf16[16,256,128]{2,1,0:T(8,128)(2,1)}, u32[]{:S(2)}) copy-start(bf16[16,256,128]{2,1,0:T(8,128)(2,1)} %copy-done) | copy-start | bytes 3145732
  37.9 0.9 copy-start.3
  38.8 0.9 copy-start.5
  39.8 0.9 copy-start.7
  64.7 25.1 %collective-permute-start.6 = (f32[4,4,32,512]{3,2,1,0:T(8,128)}, f32[4,4,32,512]{3,2,1,0:T(8,128)S(1)}, u32[]{:S(2)}, u32[]{:S(2)}) collective-permute-start(f32[4,4,32,512]{3,2,1,0:T(8,128)} %dynamic-slice_bitcast_fusion), channel_id=1, source_target_pairs={{0,4},{4,0},{8,12},{12,8},{16,20},{20,16},{24,28},{28,24},{1,5},{5... | collective-permute-start | bytes 3145736 | tf_op jit(solution)/shard_map/ppermute | solution.py:166
  90.4 12.5 %collective-permute-start.7 = (f32[4,2,32,512]{3,2,1,0:T(8,128)S(1)}, f32[4,2,32,512]{3,2,1,0:T(8,128)S(1)}, u32[]{:S(2)}, u32[]{:S(2)}) collective-permute-start(f32[4,2,32,512]{3,2,1,0:T(8,128)S(1)} %dynamic-slice_bitcast_fusion.1), channel_id=1, source_target_pairs={{0,8},{4,12},{8,0},{12,4},{16,24},{20,28},{24,16},{28,20},{1,9},{5... | collective-permute-start | bytes 1572872 | tf_op jit(solution)/shard_map/ppermute | solution.py:166
  103.2 12.5 %collective-permute-start.8 = (f32[4,1,32,512]{3,2,1,0:T(8,128)S(1)}, f32[4,1,32,512]{3,2,1,0:T(8,128)S(1)}, u32[]{:S(2)}, u32[]{:S(2)}) collective-permute-start(f32[4,1,32,512]{3,2,1,0:T(8,128)S(1)} %fusion.2), channel_id=1, source_target_pairs={{0,16},{4,20},{8,24},{12,28},{16,0},{20,4},{24,8},{28,12},{1,17},{... | collective-permute-start | bytes 786440 | tf_op jit(solution)/shard_map/ppermute | solution.py:166

commit v2 on v1

v2 whole, which is shorter than its diff:
```python
import functools
import math

import jax
import jax.numpy as jnp
from jax import lax
from jax.experimental import pallas as pl
from jax.experimental.pallas import tpu as pltpu
from jax.sharding import PartitionSpec as P

LOG2E = math.log2(math.e)
RS = 16
CS = 128
CH = 32
MU = 4096.0
POWER = 240.0 / math.log2(1.0 + MU)
MESH = pl.DeviceIdType.MESH


def encode(v):
    return jnp.exp2(jnp.log2(1.0 + MU * v) * POWER - 120.0).astype(jnp.bfloat16)


def decode(y):
    return jnp.exp2((jnp.log2(y.astype(jnp.float32)) + 120.0) * (1.0 / POWER)) * (1.0 / MU) - (1.0 / MU)


def fill_bands(dcol, drow):
    k = lax.broadcasted_iota(jnp.int32, dcol.shape, 0)
    j = lax.broadcasted_iota(jnp.int32, dcol.shape, 1)
    dcol[...] = jnp.where(k == j + CS + 1, 1.0, jnp.where(k == j + CS - 1, -1.0, 0.0)).astype(dcol.dtype)
    i = lax.broadcasted_iota(jnp.int32, drow.shape, 0)
    k = lax.broadcasted_iota(jnp.int32, drow.shape, 1)
    drow[...] = jnp.where(k == i + RS + 1, 1.0, jnp.where(k == i + RS - 1, -1.0, 0.0)).astype(drow.dtype)


def total(colors, c):
    t = jnp.full((8, 128), colors[c, 0], jnp.float32)
    for k in range(1, 4):
        t = t + colors[c, k]
    return t


def tables(layers_all, centers, widths, colors, opacity):
    scale = 1.5 / layers_all * LOG2E
    cen, quad, off = [], [], []
    mat = [[], [], []]
    for k in range(4):
        w = jnp.full((8, 128), widths[k], jnp.float32)
        o = jnp.full((8, 128), opacity[k], jnp.float32) * scale
        cen.append(jnp.full((8, 128), centers[k], jnp.float32))
        quad.append(-LOG2E / (w * w))
        off.append(jnp.log2(o))
        for c in range(3):
            mat[c].append(0.7 * colors[c, k] / o / total(colors, c))
    return cen, quad, off, mat


def march_chunk(r0, ext, cscr, rscr, dcol, drow, tab, store):
    layers = ext.shape[0] - 2
    cols = ext.shape[2] - 2 * CS
    for h in range(cols // 256):
        left = ext[1 : layers + 1, pl.ds(r0 + RS, CH), h * 256 : h * 256 + 512].reshape(layers * CH, 512)
        cscr[:, :, h * 256 : h * 256 + 256] = jnp.dot(
            left, dcol[...], preferred_element_type=jnp.float32
        ).reshape(layers, CH, 256)
    for z in range(layers):
        rscr[z] = jnp.dot(
            drow[...], ext[1 + z, pl.ds(r0, CH + 2 * RS), CS : CS + cols], preferred_element_type=jnp.float32
        )
    cen8, quad8, off8, mat8 = tab
    two = lambda v: jnp.concatenate([v, v], axis=0)
    tiles = cols // 128

    def tile(t, _):
        q0 = pl.multiple_of(t // tiles * 16, 16)
        l0 = pl.multiple_of(t % tiles * 128, 128)
        cen, quad, off = [two(v) for v in cen8], [two(v) for v in quad8], [two(v) for v in off8]
        plane = lambda z: ext[z, pl.ds(pl.multiple_of(r0 + q0 + RS, 16), 16), pl.ds(l0 + CS, 128)].astype(jnp.float32)
        acc = [jnp.zeros((16, 128), jnp.float32) for _ in range(4)]
        expo = jnp.zeros((16, 128), jnp.float32)
        passed = jnp.ones((16, 128), jnp.float32)
        before, s = plane(0), plane(1)
        for z in range(layers):
            after = plane(z + 2)
            d = after - before
            r = rscr[z, pl.ds(q0, 16), pl.ds(l0, 128)]
            c = cscr[z, pl.ds(q0, 16), pl.ds(l0, 128)]
            light = jnp.abs(d) * lax.rsqrt(d * d + r * r + (c * c + 1.0)) + (0.3 / 0.7)
            bump = []
            for k in range(4):
                u = s - cen[k]
                bump.append(jnp.exp2(u * u * quad[k] + off[k]))
            expo = expo - ((bump[0] + bump[1]) + (bump[2] + bump[3]))
            later = jnp.exp2(expo)
            weight = (passed - later) * light
            for k in range(4):
                acc[k] = acc[k] + weight * bump[k]
            passed = later
            before, s = s, after
        for ch in range(3):
            m = [two(v) for v in mat8[ch]]
            store(ch, q0, l0, (m[0] * acc[0] + m[1] * acc[1]) + (m[2] * acc[2] + m[3] * acc[3]))
        store(3, q0, l0, passed)
        return 0

    lax.fori_loop(0, CH // 16 * tiles, tile, 0)


def kernel(n, ny, nx, vol, cen, wid, col, opa, out,
           ext, part, cscr, rscr, dcol, drow, sendbuf, recvbuf,
           local_sem, depth_send, depth_recv, side_send, side_recv, row_send, row_recv, swap_send, swap_recv):
    layers, rows, cols = vol.shape
    me, iy, ix = lax.axis_index("depth"), lax.axis_index("imgy"), lax.axis_index("imgx")
    piece = rows // n
    chunks = rows // CH
    rounds = n.bit_length() - 1
    early = piece == CH

    def bit(dev, k):
        return dev // 2**k % 2

    def partner(k):
        return me + (1 - 2 * bit(me, k)) * 2**k

    def order(dev, j):
        if not early:
            return j
        half, quarter = n // 2, n // 4
        kept, i = j // half, j % half
        later, b0, b1 = i // quarter, bit(dev, 0), bit(dev, 1)
        h = 2 * ((i + b0) % quarter) + (1 - b1) * (1 - later) + b1 * later
        return 2 * h + (1 - b0) * (1 - kept) + b0 * kept

    barrier = pltpu.get_barrier_semaphore()

    def greet(dev):
        pl.semaphore_signal(barrier, inc=1, device_id=dev, device_id_type=MESH)

    for k in range(rounds):
        greet({"depth": partner(k)})
    peers = rounds
    other = me + 2 * bit(me, 0) - 1
    for name, at, there in (
        ("depth", other, jnp.logical_and(other >= 0, other < n)),
        ("imgy", iy - 1, iy > 0),
        ("imgy", iy + 1, iy < ny - 1),
        ("imgx", ix - 1, ix > 0),
        ("imgx", ix + 1, ix < nx - 1),
    ):
        pl.when(there)(lambda name=name, at=at: greet({name: at}))
        peers = peers + there.astype(jnp.int32)
    pl.semaphore_wait(barrier, peers)

    mid_z, mid_y, mid_x = pl.ds(1, layers), pl.ds(RS, rows), pl.ds(CS, cols)
    own = pltpu.make_async_copy(vol, ext.at[mid_z, mid_y, mid_x], local_sem)

    def chunk_rows(dev, j):
        return pl.multiple_of(order(dev, j) * CH, CH)

    def depth_copy(side, dev, j):
        r0 = chunk_rows(dev, j)
        return pltpu.make_async_remote_copy(
            src_ref=vol.at[pl.ds((layers - 1) * (1 - side), 1), pl.ds(r0, CH), :],
            dst_ref=ext.at[pl.ds((layers + 1) * side, 1), pl.ds(r0 + RS, CH), mid_x],
            send_sem=depth_send.at[side, j],
            recv_sem=depth_recv.at[side, j],
            device_id={"depth": me + 1 - 2 * side},
            device_id_type=MESH,
        )

    def side_copy(side, j):
        r0 = chunk_rows(me, j)
        return pltpu.make_async_remote_copy(
            src_ref=vol.at[:, pl.ds(r0, CH), pl.ds((cols - CS) * (1 - side), CS)],
            dst_ref=ext.at[mid_z, pl.ds(r0 + RS, CH), pl.ds((cols + CS) * side, CS)],
            send_sem=side_send.at[side, j],
            recv_sem=side_recv.at[side, j],
            device_id={"imgx": ix + 1 - 2 * side},
            device_id_type=MESH,
        )

    def row_copy(side):
        return pltpu.make_async_remote_copy(
            src_ref=vol.at[:, pl.ds((rows - RS) * (1 - side), RS), :],
            dst_ref=ext.at[mid_z, pl.ds((rows + RS) * side, RS), mid_x],
            send_sem=row_send.at[side],
            recv_sem=row_recv.at[side],
            device_id={"imgy": iy + 1 - 2 * side},
            device_id_type=MESH,
        )

    sends = (me < n - 1, me > 0)
    side_sends = (ix < nx - 1, ix > 0)
    row_sends = (iy < ny - 1, iy > 0)

    def start_halos(j):
        for s in range(2):
            pl.when(side_sends[s])(lambda s=s: side_copy(s, j).start())
            pl.when(sends[s])(lambda s=s: depth_copy(s, me + 1 - 2 * s, j).start())

    start_halos(0)
    own.start()
    for s in range(2):
        pl.when(row_sends[s])(lambda s=s: row_copy(s).start())

    def rest(j, _):
        start_halos(j)
        return 0

    lax.fori_loop(1, chunks, rest, 0)

    def clear(region):
        region[...] = jnp.zeros(region.shape, region.dtype)

    for s in range(2):
        pl.when(jnp.logical_not(sends[1 - s]))(lambda s=s: clear(ext.at[pl.ds((layers + 1) * s, 1), mid_y, mid_x]))
        pl.when(jnp.logical_not(side_sends[1 - s]))(
            lambda s=s: clear(ext.at[mid_z, mid_y, pl.ds((cols + CS) * s, CS)]))
        pl.when(jnp.logical_not(row_sends[1 - s]))(
            lambda s=s: clear(ext.at[mid_z, pl.ds((rows + RS) * s, RS), mid_x]))
    fill_bands(dcol, drow)
    tab = tables(layers * n, cen, wid, col, opa)
    own.wait()

    lanes = cols // 128

    def swap_copy(k, h):
        slot = n - n // 2**k + h
        return pltpu.make_async_remote_copy(
            src_ref=sendbuf.at[slot],
            dst_ref=recvbuf.at[slot],
            send_sem=swap_send.at[slot],
            recv_sem=swap_recv.at[slot],
            device_id={"depth": partner(k)},
            device_id_type=MESH,
        )

    def send_piece(p, k):
        h = p // 2 ** (k + 1)
        slot = n - n // 2**k + h
        r0 = pl.multiple_of(p * piece, piece)

        def tile(t, _):
            here = pl.ds(pl.multiple_of(t * 128, 128), 128)
            for ch in range(4):
                v = part[ch, pl.ds(r0, piece), here]
                sendbuf[slot, ch, :, here] = encode(1.0 - v if ch == 3 else v)
            return 0

        lax.fori_loop(0, lanes, tile, 0)
        swap_copy(k, h).start()

    def merge_piece(p, k, last):
        h = p // 2 ** (k + 1)
        slot = n - n // 2**k + h
        r0 = pl.multiple_of(p * piece, piece)
        swap_copy(k, h).wait_recv()
        behind = bit(me, k) == 1

        def tile(t, _):
            here = pl.ds(pl.multiple_of(t * 128, 128), 128)
            mine = [part[ch, pl.ds(r0, piece), here] for ch in range(4)]
            got = [decode(recvbuf[slot, ch, :, here]) for ch in range(4)]
            got[3] = 1.0 - got[3]
            near_t = jnp.where(behind, got[3], mine[3])
            merged = [jnp.where(behind, got[c], mine[c]) + near_t * jnp.where(behind, mine[c], got[c]) for c in range(3)]
            merged.append(mine[3] * got[3])
            for ch in range(4):
                if last:
                    v = 1.0 - merged[3] if ch == 3 else merged[ch] * total(col, ch)[:1]
                    out[ch, 0, :, here] = v
                else:
                    part[ch, pl.ds(r0, piece), here] = merged[ch]
            return 0

        lax.fori_loop(0, lanes, tile, 0)

    def chunk(j, _):
        p = order(me, j)
        r0 = pl.multiple_of(p * CH, CH)
        for s in range(2):
            pl.when(sends[1 - s])(lambda s=s: depth_copy(s, me, j).wait_recv())
            pl.when(side_sends[1 - s])(lambda s=s: side_copy(s, j).wait_recv())
            edge = p == (chunks - 1) * s
            pl.when(jnp.logical_and(row_sends[1 - s], edge))(lambda s=s: row_copy(s).wait_recv())

        def store(ch, q0, l0, value):
            part[ch, pl.ds(pl.multiple_of(r0 + q0, 16), 16), pl.ds(l0, 128)] = value

        march_chunk(r0, ext, cscr, rscr, dcol, drow, tab, store)
        if early:
            pl.when(j < n // 2)(lambda: send_piece(p, 0))
        return 0

    lax.fori_loop(0, chunks, chunk, 0)

    for k in range(rounds):

        def give(h, _, k=k):
            p = me % 2**k + (1 - bit(me, k)) * 2**k + h * 2 ** (k + 1)
            for done in range(k):
                merge_piece(p, done, False)
            send_piece(p, k)
            return 0

        if k > 0 or not early:
            lax.fori_loop(0, n // 2 ** (k + 1), give, 0)
    for k in range(rounds):
        merge_piece(me, k, k == rounds - 1)

    def finish(j, _):
        for s in range(2):
            pl.when(side_sends[s])(lambda s=s: side_copy(s, j).wait_send())
            pl.when(sends[s])(lambda s=s: depth_copy(s, me + 1 - 2 * s, j).wait_send())
        return 0

    lax.fori_loop(0, chunks, finish, 0)
    for s in range(2):
        pl.when(row_sends[s])(lambda s=s: row_copy(s).wait_send())
    for k in range(rounds):

        def sent(h, _, k=k):
            swap_copy(k, h).wait_send()
            return 0

        lax.fori_loop(0, n // 2 ** (k + 1), sent, 0)


def local(volume, cen, wid, col, opa):
    n, ny, nx = lax.axis_size("depth"), lax.axis_size("imgy"), lax.axis_size("imgx")
    layers, rows, cols = volume.shape
    piece = rows // n
    smem = pl.BlockSpec(memory_space=pltpu.SMEM)
    dma = pltpu.SemaphoreType.DMA
    return pl.pallas_call(
        functools.partial(kernel, n, ny, nx),
        out_shape=jax.ShapeDtypeStruct((4, 1, piece, cols), jnp.float32),
        in_specs=[pl.BlockSpec(memory_space=pl.ANY)] + [smem] * 4,
        out_specs=pl.BlockSpec(memory_space=pltpu.VMEM),
        scratch_shapes=[
            pltpu.VMEM((layers + 2, rows + 2 * RS, cols + 2 * CS), jnp.bfloat16),
            pltpu.VMEM((4, rows, cols), jnp.float32),
            pltpu.VMEM((layers, CH, cols), jnp.float32),
            pltpu.VMEM((layers, CH, cols), jnp.float32),
            pltpu.VMEM((512, 256), jnp.bfloat16),
            pltpu.VMEM((CH, CH + 2 * RS), jnp.bfloat16),
            pltpu.VMEM((n - 1, 4, piece, cols), jnp.bfloat16),
            pltpu.VMEM((n - 1, 4, piece, cols), jnp.bfloat16),
            dma,
            dma((2, rows // CH)),
            dma((2, rows // CH)),
            dma((2, rows // CH)),
            dma((2, rows // CH)),
            dma((2,)),
            dma((2,)),
            dma((n - 1,)),
            dma((n - 1,)),
        ],
        compiler_params=pltpu.CompilerParams(
            vmem_limit_bytes=48 * 2**20, collective_id=0, has_side_effects=True
        ),
        name="march_swap",
    )(volume, cen, wid, col, opa)


def solution(mesh):
    return jax.shard_map(
        local,
        mesh=mesh,
        in_specs=(P("depth", "imgy", "imgx"), P(), P(), P(), P()),
        out_specs=P(None, "imgy", "depth", "imgx"),
        check_vma=False,
    )
```

time: 117 us -> 53.7 us (0.46)
  waiting for transfers between devices: 57 us -> 0 us
  Pallas kernels: 22.8 us -> 47.9 us
  starting transfers between devices: 20.5 us -> 0 us
  local copies, waits for them, and re-layouts: 14.4 us -> 5.54 us
  other arithmetic: 1.66 us -> 0 us
    ppermute x9 -> x0, waiting for transfers between devices: 57 us -> none  [the longest x3 43.6 us: local(): got = lax.ppermute(sent, 'depth', [(i, i ^ 1 << bit) for i in range(slabs)])]
    pallas_call x1, Pallas kernels: 22.8 us -> 47.9 us  [local(): pl.pallas_call(functools.partial(kernel, n, ny, nx), out_shape=jax.ShapeD...]
    ppermute x9 -> x0, starting transfers between devices: 20.5 us -> none  [the longest x6 13.9 us: shifted(): return lax.ppermute(block, axis, pairs)]
    slice x3 -> x0, local copies, waits for them, and re-layouts: 6.12 us -> none  [the longest x1 3.18 us: local(): right = shifted(volume[:, :, :CS], 'imgx', False)]
    unnamed x24 -> x11, local copies, waits for them, and re-layouts: 7.17 us -> 5.54 us
  transfers between devices with their start and end apart: 9 -> 0, of which waited for: 5 -> 0; matrix products, arithmetic and copies ran while one was open for 3% -> 0% of each run, Pallas kernels for 0% -> 0%
where the time goes in v2:
time: 53.7 us; the launch traced here: 53.5 us
  Pallas kernels  47.9 us (89%)
  local copies, waits for them, and re-layouts  5.54 us (10%)
    pallas_call x1, Pallas kernels, local(): pl.pallas_call(functools.partial(kernel, n, ny, nx), out_shape=jax.ShapeD...  47.9 us
    unnamed x11, local copies, waits for them, and re-layouts  5.54 us

profile of v2, /device:TPU:0, one launch (start us, length us, event | category | flops | bytes accessed | tf_op | source)
XLA Modules:
  0.0 53.5 jit_solution(8347379296553455864)
XLA Ops:
  0.0 0.0 copy-start
  0.0 2.2 %copy-done = bf16[16,256,512]{2,1,0:T(8,128)(2,1)S(1)} copy-done((bf16[16,256,512]{2,1,0:T(8,128)(2,1)S(1)}, bf16[16,256,512]{2,1,0:T(8,128)(2,1)}, u32[]{:S(2)}) %copy-start) | copy-done | bytes 4194328
  2.2 0.0 copy-start.1
  2.2 0.7 %copy-done.1 = f32[3,4]{1,0:T(4,128)S(1)} copy-done((f32[3,4]{1,0:T(4,128)S(1)}, f32[3,4]{1,0:T(4,128)}, u32[]{:S(2)}) %copy-start.1) | copy-done | bytes 72
  2.9 0.0 copy-start.2
  2.9 0.7 %copy-done.2 = f32[4]{0:T(128)S(1)} copy-done((f32[4]{0:T(128)S(1)}, f32[4]{0:T(128)}, u32[]{:S(2)}) %copy-start.2) | copy-done | bytes 40
  3.5 0.0 copy-start.3
  3.5 0.7 %copy-done.3 = f32[4]{0:T(128)S(1)} copy-done((f32[4]{0:T(128)S(1)}, f32[4]{0:T(128)}, u32[]{:S(2)}) %copy-start.3) | copy-done | bytes 40
  4.2 0.0 copy-start.4
  4.2 0.7 %copy-done.4 = f32[4]{0:T(128)S(1)} copy-done((f32[4]{0:T(128)S(1)}, f32[4]{0:T(128)}, u32[]{:S(2)}) %copy-start.4) | copy-done | bytes 40
  4.8 47.9 %march_swap.1 = f32[4,1,32,512]{3,2,1,0:T(8,128)S(1)} custom-call(bf16[16,256,512]{2,1,0:T(8,128)(2,1)S(1)} %copy-done, f32[4]{0:T(128)S(1)} %copy-done.2, f32[4]{0:T(128)S(1)} %copy-done.3, f32[3,4]{1,0:T(4,128)S(1)} %copy-done.1, f32[4]{0:T(128)S(1)} %copy-done.4), custom_call_target="tpu_custom_call" | custom-call | tf_op jit(solution)/shard_map/march_swap/pallas_call | solution.py:336
  52.8 0.7 %copy.7 = f32[4,1,32,512]{3,2,1,0:T(8,128)} copy(f32[4,1,32,512]{3,2,1,0:T(8,128)S(1)} %march_swap.1) | data formatting | bytes 524288
Async XLA Ops:
  0.0 2.2 %copy-start = (bf16[16,256,512]{2,1,0:T(8,128)(2,1)S(1)}, bf16[16,256,512]{2,1,0:T(8,128)(2,1)}, u32[]{:S(2)}) copy-start(bf16[16,256,512]{2,1,0:T(8,128)(2,1)} %vol.1) | copy-start | bytes 12582916
  2.2 0.7 %copy-start.1 = (f32[3,4]{1,0:T(4,128)S(1)}, f32[3,4]{1,0:T(4,128)}, u32[]{:S(2)}) copy-start(f32[3,4]{1,0:T(4,128)} %col.1) | copy-start | bytes 148
  2.9 0.7 %copy-start.2 = (f32[4]{0:T(128)S(1)}, f32[4]{0:T(128)}, u32[]{:S(2)}) copy-start(f32[4]{0:T(128)} %cen.1) | copy-start | bytes 52
  3.5 0.7 %copy-start.3 = (f32[4]{0:T(128)S(1)}, f32[4]{0:T(128)}, u32[]{:S(2)}) copy-start(f32[4]{0:T(128)} %wid.1) | copy-start | bytes 52
  4.2 0.7 %copy-start.4 = (f32[4]{0:T(128)S(1)}, f32[4]{0:T(128)}, u32[]{:S(2)}) copy-start(f32[4]{0:T(128)} %opa.1) | copy-start | bytes 52

commit v3 on v2

--- a/solution.py
+++ b/solution.py
@@ -12,6 +12,7 @@
 RS = 16
 CS = 128
 CH = 32
+AHEAD = 3
 MU = 4096.0
 POWER = 240.0 / math.log2(1.0 + MU)
 MESH = pl.DeviceIdType.MESH
@@ -107,9 +108,9 @@
     lax.fori_loop(0, CH // 16 * tiles, tile, 0)
 
 
-def kernel(n, ny, nx, vol, cen, wid, col, opa, out,
+def kernel(n, ny, nx, vol, cen_h, wid_h, col_h, opa_h, out, cen, wid, col, opa,
            ext, part, cscr, rscr, dcol, drow, sendbuf, recvbuf,
-           local_sem, depth_send, depth_recv, side_send, side_recv, row_send, row_recv, swap_send, swap_recv):
+           local_sem, fetch_sem, depth_send, depth_recv, side_send, side_recv, row_send, row_recv, swap_send, swap_recv):
     layers, rows, cols = vol.shape
     me, iy, ix = lax.axis_index("depth"), lax.axis_index("imgy"), lax.axis_index("imgx")
     piece = rows // n
@@ -126,11 +127,13 @@
     def order(dev, j):
         if not early:
             return j
-        half, quarter = n // 2, n // 4
-        kept, i = j // half, j % half
-        later, b0, b1 = i // quarter, bit(dev, 0), bit(dev, 1)
-        h = 2 * ((i + b0) % quarter) + (1 - b1) * (1 - later) + b1 * later
-        return 2 * h + (1 - b0) * (1 - kept) + b0 * kept
+        edge = (dev % (n - 1) == 0).astype(jnp.int32) * (j < 2).astype(jnp.int32)
+        j = j + edge * (1 - 2 * j)
+        p = 0
+        for k in range(rounds):
+            a, b = bit(dev, k), 1 - bit(j, rounds - 1 - k)
+            p = p + 2**k * (a + b - 2 * a * b)
+        return p
 
     barrier = pltpu.get_barrier_semaphore()
 
@@ -153,6 +156,8 @@
     pl.semaphore_wait(barrier, peers)
 
     mid_z, mid_y, mid_x = pl.ds(1, layers), pl.ds(RS, rows), pl.ds(CS, cols)
+    fetches = [pltpu.make_async_copy(a, b, fetch_sem.at[i]) for i, (a, b) in enumerate(
+        ((cen_h, cen), (wid_h, wid), (col_h, col), (opa_h, opa)))]
     own = pltpu.make_async_copy(vol, ext.at[mid_z, mid_y, mid_x], local_sem)
 
     def chunk_rows(dev, j):
@@ -199,8 +204,10 @@
             pl.when(side_sends[s])(lambda s=s: side_copy(s, j).start())
             pl.when(sends[s])(lambda s=s: depth_copy(s, me + 1 - 2 * s, j).start())
 
-    start_halos(0)
+    start_halos(jnp.int32(0))
     own.start()
+    for copy in fetches:
+        copy.start()
     for s in range(2):
         pl.when(row_sends[s])(lambda s=s: row_copy(s).start())
 
@@ -208,7 +215,7 @@
         start_halos(j)
         return 0
 
-    lax.fori_loop(1, chunks, rest, 0)
+    lax.fori_loop(1, AHEAD, rest, 0)
 
     def clear(region):
         region[...] = jnp.zeros(region.shape, region.dtype)
@@ -220,6 +227,8 @@
         pl.when(jnp.logical_not(row_sends[1 - s]))(
             lambda s=s: clear(ext.at[mid_z, pl.ds((rows + RS) * s, RS), mid_x]))
     fill_bands(dcol, drow)
+    for copy in fetches:
+        copy.wait()
     tab = tables(layers * n, cen, wid, col, opa)
     own.wait()
 
@@ -276,9 +285,15 @@
 
         lax.fori_loop(0, lanes, tile, 0)
 
+    def give_piece(p, k):
+        for done in range(k):
+            merge_piece(p, done, False)
+        send_piece(p, k)
+
     def chunk(j, _):
         p = order(me, j)
         r0 = pl.multiple_of(p * CH, CH)
+        pl.when(j + AHEAD < chunks)(lambda: start_halos(j + AHEAD))
         for s in range(2):
             pl.when(sends[1 - s])(lambda s=s: depth_copy(s, me, j).wait_recv())
             pl.when(side_sends[1 - s])(lambda s=s: side_copy(s, j).wait_recv())
@@ -290,21 +305,20 @@
 
         march_chunk(r0, ext, cscr, rscr, dcol, drow, tab, store)
         if early:
-            pl.when(j < n // 2)(lambda: send_piece(p, 0))
+            for k in range(rounds):
+                mine = jnp.logical_and(j >= n - n // 2**k, j < n - n // 2 ** (k + 1))
+                pl.when(mine)(lambda k=k: give_piece(p, k))
         return 0
 
     lax.fori_loop(0, chunks, chunk, 0)
 
-    for k in range(rounds):
-
-        def give(h, _, k=k):
-            p = me % 2**k + (1 - bit(me, k)) * 2**k + h * 2 ** (k + 1)
-            for done in range(k):
-                merge_piece(p, done, False)
-            send_piece(p, k)
-            return 0
-
-        if k > 0 or not early:
+    if not early:
+        for k in range(rounds):
+
+            def give(h, _, k=k):
+                give_piece(me % 2**k + (1 - bit(me, k)) * 2**k + h * 2 ** (k + 1), k)
+                return 0
+
             lax.fori_loop(0, n // 2 ** (k + 1), give, 0)
     for k in range(rounds):
         merge_piece(me, k, k == rounds - 1)
@@ -331,14 +345,14 @@
     n, ny, nx = lax.axis_size("depth"), lax.axis_size("imgy"), lax.axis_size("imgx")
     layers, rows, cols = volume.shape
     piece = rows // n
-    smem = pl.BlockSpec(memory_space=pltpu.SMEM)
     dma = pltpu.SemaphoreType.DMA
     return pl.pallas_call(
         functools.partial(kernel, n, ny, nx),
         out_shape=jax.ShapeDtypeStruct((4, 1, piece, cols), jnp.float32),
-        in_specs=[pl.BlockSpec(memory_space=pl.ANY)] + [smem] * 4,
+        in_specs=[pl.BlockSpec(memory_space=pltpu.HBM)] * 5,
         out_specs=pl.BlockSpec(memory_space=pltpu.VMEM),
         scratch_shapes=[
+            *(pltpu.SMEM(a.shape, jnp.float32) for a in (cen, wid, col, opa)),
             pltpu.VMEM((layers + 2, rows + 2 * RS, cols + 2 * CS), jnp.bfloat16),
             pltpu.VMEM((4, rows, cols), jnp.float32),
             pltpu.VMEM((layers, CH, cols), jnp.float32),
@@ -348,6 +362,7 @@
             pltpu.VMEM((n - 1, 4, piece, cols), jnp.bfloat16),
             pltpu.VMEM((n - 1, 4, piece, cols), jnp.bfloat16),
             dma,
+            dma((4,)),
             dma((2, rows // CH)),
             dma((2, rows // CH)),
             dma((2, rows // CH)),

time: 53.7 us -> 43.9 us (0.82)
  Pallas kernels: 47.9 us -> 38.2 us
    pallas_call x1, Pallas kernels: 47.9 us -> 38.2 us  [local(): pl.pallas_call(functools.partial(kernel, n, ny, nx), out_shape=jax.ShapeD...]
where the time goes in v3:
time: 43.9 us; the launch traced here: 43.7 us
  Pallas kernels  38.2 us (87%)
  local copies, waits for them, and re-layouts  5.54 us (13%)
    pallas_call x1, Pallas kernels, local(): pl.pallas_call(functools.partial(kernel, n, ny, nx), out_shape=jax.ShapeD...  38.2 us
    unnamed x11, local copies, waits for them, and re-layouts  5.54 us

profile of v3, /device:TPU:0, one launch (start us, length us, event | category | flops | bytes accessed | tf_op | source)
XLA Modules:
  0.0 43.7 jit_solution(8145601170215549816)
XLA Ops:
  0.0 0.0 copy-start
  0.0 2.2 %copy-done = bf16[16,256,512]{2,1,0:T(8,128)(2,1)S(1)} copy-done((bf16[16,256,512]{2,1,0:T(8,128)(2,1)S(1)}, bf16[16,256,512]{2,1,0:T(8,128)(2,1)}, u32[]{:S(2)}) %copy-start) | copy-done | bytes 4194328
  2.2 0.0 copy-start.1
  2.2 0.7 %copy-done.1 = f32[3,4]{1,0:T(4,128)S(1)} copy-done((f32[3,4]{1,0:T(4,128)S(1)}, f32[3,4]{1,0:T(4,128)}, u32[]{:S(2)}) %copy-start.1) | copy-done | bytes 72
  2.9 0.0 copy-start.2
  2.9 0.7 %copy-done.2 = f32[4]{0:T(128)S(1)} copy-done((f32[4]{0:T(128)S(1)}, f32[4]{0:T(128)}, u32[]{:S(2)}) %copy-start.2) | copy-done | bytes 40
  3.5 0.0 copy-start.3
  3.5 0.7 %copy-done.3 = f32[4]{0:T(128)S(1)} copy-done((f32[4]{0:T(128)S(1)}, f32[4]{0:T(128)}, u32[]{:S(2)}) %copy-start.3) | copy-done | bytes 40
  4.2 0.0 copy-start.4
  4.2 0.7 %copy-done.4 = f32[4]{0:T(128)S(1)} copy-done((f32[4]{0:T(128)S(1)}, f32[4]{0:T(128)}, u32[]{:S(2)}) %copy-start.4) | copy-done | bytes 40
  4.8 38.2 %march_swap.1 = f32[4,1,32,512]{3,2,1,0:T(8,128)S(1)} custom-call(bf16[16,256,512]{2,1,0:T(8,128)(2,1)S(1)} %copy-done, f32[4]{0:T(128)S(1)} %copy-done.2, f32[4]{0:T(128)S(1)} %copy-done.3, f32[3,4]{1,0:T(4,128)S(1)} %copy-done.1, f32[4]{0:T(128)S(1)} %copy-done.4), custom_call_target="tpu_custom_call" | custom-call | tf_op jit(solution)/shard_map/march_swap/pallas_call | solution.py:349
  43.0 0.7 %copy.7 = f32[4,1,32,512]{3,2,1,0:T(8,128)} copy(f32[4,1,32,512]{3,2,1,0:T(8,128)S(1)} %march_swap.1) | data formatting | bytes 524288
Async XLA Ops:
  0.0 2.2 %copy-start = (bf16[16,256,512]{2,1,0:T(8,128)(2,1)S(1)}, bf16[16,256,512]{2,1,0:T(8,128)(2,1)}, u32[]{:S(2)}) copy-start(bf16[16,256,512]{2,1,0:T(8,128)(2,1)} %vol.1) | copy-start | bytes 12582916
  2.2 0.7 %copy-start.1 = (f32[3,4]{1,0:T(4,128)S(1)}, f32[3,4]{1,0:T(4,128)}, u32[]{:S(2)}) copy-start(f32[3,4]{1,0:T(4,128)} %col_h.1) | copy-start | bytes 148
  2.9 0.7 %copy-start.2 = (f32[4]{0:T(128)S(1)}, f32[4]{0:T(128)}, u32[]{:S(2)}) copy-start(f32[4]{0:T(128)} %cen_h.1) | copy-start | bytes 52
  3.5 0.7 %copy-start.3 = (f32[4]{0:T(128)S(1)}, f32[4]{0:T(128)}, u32[]{:S(2)}) copy-start(f32[4]{0:T(128)} %wid_h.1) | copy-start | bytes 52
  4.2 0.7 %copy-start.4 = (f32[4]{0:T(128)S(1)}, f32[4]{0:T(128)}, u32[]{:S(2)}) copy-start(f32[4]{0:T(128)} %opa_h.1) | copy-start | bytes 52

commit v4 on v3

--- a/solution.py
+++ b/solution.py
@@ -373,7 +373,7 @@
             dma((n - 1,)),
         ],
         compiler_params=pltpu.CompilerParams(
-            vmem_limit_bytes=48 * 2**20, collective_id=0, has_side_effects=True
+            vmem_limit_bytes=64 * 2**20, collective_id=0, has_side_effects=True
         ),
         name="march_swap",
     )(volume, cen, wid, col, opa)

time: 43.9 us -> 40.6 us (0.925)
  local copies, waits for them, and re-layouts: 5.54 us -> 1.67 us
  Pallas kernels: 38.2 us -> 38.7 us
    unnamed x11 -> x1, local copies, waits for them, and re-layouts: 5.54 us -> 1.67 us
    pallas_call x1, Pallas kernels: 38.2 us -> 38.7 us  [local(): pl.pallas_call(functools.partial(kernel, n, ny, nx), out_shape=jax.ShapeD...]
where the time goes in v4:
time: 40.6 us; the launch traced here: 40.4 us
  Pallas kernels  38.7 us (95%)
  local copies, waits for them, and re-layouts  1.67 us (4%)
    pallas_call x1, Pallas kernels, local(): pl.pallas_call(functools.partial(kernel, n, ny, nx), out_shape=jax.ShapeD...  38.7 us
    unnamed x1, local copies, waits for them, and re-layouts  1.67 us

profile of v4, /device:TPU:0, one launch (start us, length us, event | category | flops | bytes accessed | tf_op | source)
XLA Modules:
  0.0 40.4 jit_solution(10763724169973762099)
XLA Ops:
  0.0 38.7 %march_swap.1 = f32[4,1,32,512]{3,2,1,0:T(8,128)} custom-call(bf16[16,256,512]{2,1,0:T(8,128)(2,1)} %vol.1, f32[4]{0:T(128)} %cen_h.1, f32[4]{0:T(128)} %wid_h.1, f32[3,4]{1,0:T(4,128)} %col_h.1, f32[4]{0:T(128)} %opa_h.1), custom_call_target="tpu_custom_call" | custom-call | tf_op jit(solution)/shard_map/march_swap/pallas_call | solution.py:349
  38.7 1.7 %copy.7 = f32[4,1,32,512]{3,2,1,0:T(8,128)} copy(f32[4,1,32,512]{3,2,1,0:T(8,128)} %march_swap.1) | data formatting | bytes 524288

commit v5 on v4

--- a/solution.py
+++ b/solution.py
@@ -57,7 +57,7 @@
     return cen, quad, off, mat
 
 
-def march_chunk(r0, ext, cscr, rscr, dcol, drow, tab, store):
+def march_chunk(r0, ext, cscr, rscr, dcol, drow, tab, ready, store):
     layers = ext.shape[0] - 2
     cols = ext.shape[2] - 2 * CS
     for h in range(cols // 256):
@@ -69,6 +69,7 @@
         rscr[z] = jnp.dot(
             drow[...], ext[1 + z, pl.ds(r0, CH + 2 * RS), CS : CS + cols], preferred_element_type=jnp.float32
         )
+    ready()
     cen8, quad8, off8, mat8 = tab
     two = lambda v: jnp.concatenate([v, v], axis=0)
     tiles = cols // 128
@@ -105,7 +106,7 @@
         store(3, q0, l0, passed)
         return 0
 
-    lax.fori_loop(0, CH // 16 * tiles, tile, 0)
+    lax.fori_loop(0, CH // 16 * tiles, tile, 0, unroll=2)
 
 
 def kernel(n, ny, nx, vol, cen_h, wid_h, col_h, opa_h, out, cen, wid, col, opa,
@@ -295,15 +296,18 @@
         r0 = pl.multiple_of(p * CH, CH)
         pl.when(j + AHEAD < chunks)(lambda: start_halos(j + AHEAD))
         for s in range(2):
-            pl.when(sends[1 - s])(lambda s=s: depth_copy(s, me, j).wait_recv())
             pl.when(side_sends[1 - s])(lambda s=s: side_copy(s, j).wait_recv())
             edge = p == (chunks - 1) * s
             pl.when(jnp.logical_and(row_sends[1 - s], edge))(lambda s=s: row_copy(s).wait_recv())
 
+        def ready():
+            for s in range(2):
+                pl.when(sends[1 - s])(lambda s=s: depth_copy(s, me, j).wait_recv())
+
         def store(ch, q0, l0, value):
             part[ch, pl.ds(pl.multiple_of(r0 + q0, 16), 16), pl.ds(l0, 128)] = value
 
-        march_chunk(r0, ext, cscr, rscr, dcol, drow, tab, store)
+        march_chunk(r0, ext, cscr, rscr, dcol, drow, tab, ready, store)
         if early:
             for k in range(rounds):
                 mine = jnp.logical_and(j >= n - n // 2**k, j < n - n // 2 ** (k + 1))

time: 40.6 us -> 39.4 us (0.970)
  Pallas kernels: 38.7 us -> 37.6 us
    pallas_call x1, Pallas kernels: 38.7 us -> 37.6 us  [local(): pl.pallas_call(functools.partial(kernel, n, ny, nx), out_shape=jax.ShapeD...]
where the time goes in v5:
time: 39.4 us; the launch traced here: 39.3 us
  Pallas kernels  37.6 us (95%)
  local copies, waits for them, and re-layouts  1.67 us (4%)
    pallas_call x1, Pallas kernels, local(): pl.pallas_call(functools.partial(kernel, n, ny, nx), out_shape=jax.ShapeD...  37.6 us
    unnamed x1, local copies, waits for them, and re-layouts  1.67 us

profile of v5, /device:TPU:0, one launch (start us, length us, event | category | flops | bytes accessed | tf_op | source)
XLA Modules:
  0.0 39.3 jit_solution(10879713986447459060)
XLA Ops:
  0.0 37.6 %march_swap.1 = f32[4,1,32,512]{3,2,1,0:T(8,128)} custom-call(bf16[16,256,512]{2,1,0:T(8,128)(2,1)} %vol.1, f32[4]{0:T(128)} %cen_h.1, f32[4]{0:T(128)} %wid_h.1, f32[3,4]{1,0:T(4,128)} %col_h.1, f32[4]{0:T(128)} %opa_h.1), custom_call_target="tpu_custom_call" | custom-call | tf_op jit(solution)/shard_map/march_swap/pallas_call | solution.py:353
  37.6 1.7 %copy.7 = f32[4,1,32,512]{3,2,1,0:T(8,128)} copy(f32[4,1,32,512]{3,2,1,0:T(8,128)} %march_swap.1) | data formatting | bytes 524288
